TPU v7x, 32 devices: a whole 2x2x4 slice. The times are simulated.
32 devices in a mesh: dp: 16 (over z, x, core), tensor: 2 (over y).
Axes of the slice: x: 2, y: 2, z: 4, core: 2. Of those that a mesh axis runs over, the one named last changes fastest.
Arguments:
- tokens: bfloat16 [32768, 512], P('dp'), may hold values from -6 to 6
- seq_lengths: int32 [32], P('dp'), may hold values from 1024 to 1024, as said below
- packed_slot: int32 [32768], P('dp'), may hold values from 0 to 32767, as said below
- out_grad: bfloat16 [32768, 512], P('dp'), may hold values from -6 to 6
- qkv_weight: bfloat16 [3, 512, 512], P(None, None, 'tensor'), may hold values from -0.25 to 0.25
- out_weight: bfloat16 [512, 512], P('tensor'), may hold values from -2 to 2
- up_weight: bfloat16 [512, 2048], P(None, 'tensor'), may hold values from -0.25 to 0.25
- down_weight: bfloat16 [2048, 512], P('tensor'), may hold values from -0.125 to 0.125
- gain_first: float32 [512], replicated, may hold values from 0.1 to 1.9
- shift_first: float32 [512], replicated, may hold values from -0.6 to 0.6
- gain_second: float32 [512], replicated, may hold values from 0.1 to 1.9
- shift_second: float32 [512], replicated, may hold values from -0.6 to 0.6
- up_bias: float32 [2048], P('tensor'), may hold values from -12 to 12
Outputs:
- layer_out: bfloat16 [32768, 512], P('dp')
- grad_input: bfloat16 [32768, 512], P('dp')
- grad_qkv: float32 [3, 512, 512], P(None, None, 'tensor')
- grad_outproj: float32 [512, 512], P('tensor')
- grad_up: float32 [512, 2048], P(None, 'tensor')
- grad_down: float32 [2048, 512], P('tensor')
- grad_gain_first: float32 [512], replicated
- grad_shift_first: float32 [512], replicated
- grad_gain_second: float32 [512], replicated
- grad_shift_second: float32 [512], replicated
- grad_up_bias: float32 [2048], P('tensor')
Inputs may be any that keep to these rules, and one draw needn't show every extreme that they name: Each pair seq_lengths[2b], seq_lengths[2b+1] sums to 2048; every length is a multiple of 64; some pair is (1024, 1024). packed_slot is a permutation of the rows; of the 2048 rows of one index of dp, exactly 128 have packed_slot // 2048 equal to each index of dp.
All inputs are finite; a program needn't handle non-finite values.
Results may differ from a plain program's by a relative error of at most 0.015.
Values may be sent and summed in bfloat16 or wider, within the bound.
No kernel may reach another device: no remote copies, remote signals or barrier semaphores. Data moves between devices by JAX's collectives and lax.ppermute only.
A program may use at most 192 MiB of HBM per device.

v0:
```python
import jax
import jax.numpy as jnp
from jax import lax
from jax.sharding import PartitionSpec as P

HD = 64
BLK = 64


def layer_norm(value, gain, shift):
    mean = jnp.mean(value, axis=-1, keepdims=True)
    cent = value - mean
    var = jnp.mean(cent * cent, axis=-1, keepdims=True)
    return cent * lax.rsqrt(var + 1e-05) * gain + shift


def feature(value):
    return jnp.where(value > 0, value + 1.0, jnp.exp(jnp.minimum(value, 0.0)))


def feature_slope(value):
    return jnp.where(value > 0, 1.0, jnp.exp(jnp.minimum(value, 0.0)))


def silu_slope(value):
    sigma = jax.nn.sigmoid(value)
    return sigma * (1.0 + value * (1.0 - sigma))


def rounded(value):
    return lax.optimization_barrier(value.astype(jnp.bfloat16)).astype(jnp.float32)


def linear_attention(q_feat, k_feat, v_feat, stretch_seq):
    best = lax.Precision.HIGHEST
    nblk = q_feat.shape[0] // BLK
    query = q_feat.reshape(nblk, BLK, -1, HD)
    keys = k_feat.reshape(nblk, BLK, -1, HD)
    values = v_feat.reshape(nblk, BLK, -1, HD)
    outer = jnp.einsum("cjhe,cjhf->chef", keys, values, precision=best)
    ksum = jnp.sum(keys, axis=1)
    index = jnp.arange(nblk)
    mixing = (
        (index[None, :] < index[:, None]) & (stretch_seq[None, :] == stretch_seq[:, None])
    ).astype(jnp.float32)
    state = jnp.einsum("cd,dhef->chef", mixing, outer, precision=best)
    zsum = jnp.einsum("cd,dhe->che", mixing, ksum, precision=best)
    scores = jnp.einsum("cihe,cjhe->chij", query, keys, precision=best)
    lower = (jnp.arange(BLK)[None, :] <= jnp.arange(BLK)[:, None]).astype(jnp.float32)
    scores = scores * lower
    numer = jnp.einsum("cihe,chef->cihf", query, state, precision=best)
    numer = numer + jnp.einsum("chij,cjhf->cihf", scores, values, precision=best)
    denom = jnp.einsum("cihe,che->cih", query, zsum, precision=best)
    denom = denom + jnp.transpose(jnp.sum(scores, axis=-1), (0, 2, 1)) + 1e-06
    result = numer / denom[..., None]
    return result.reshape(nblk * BLK, -1)


def per_device(
    tokens,
    seq_lengths,
    packed_slot,
    out_grad,
    qkv_weight,
    out_weight,
    up_weight,
    down_weight,
    gain_first,
    shift_first,
    gain_second,
    shift_second,
    up_bias,
):
    rows = tokens.shape[0]
    count = lax.axis_size("dp")
    slot = rows // count
    order = jnp.argsort(packed_slot)
    sent = (
        tokens[order].reshape(count, slot, -1),
        out_grad[order].reshape(count, slot, -1),
        packed_slot[order].reshape(count, slot),
    )
    got_rows, got_grads, got_slots = (
        lax.all_to_all(sent[0], "dp", split_axis=0, concat_axis=0, tiled=True),
        lax.all_to_all(sent[1], "dp", split_axis=0, concat_axis=0, tiled=True),
        lax.all_to_all(sent[2], "dp", split_axis=0, concat_axis=0, tiled=True),
    )
    local_pos = got_slots.reshape(rows) % rows
    arrange = jnp.argsort(local_pos)
    inputs = got_rows.reshape(rows, -1)[arrange].astype(jnp.float32)
    grad_low = got_grads.reshape(rows, -1)[arrange]
    nblk = rows // BLK
    stretch_seq = (jnp.arange(nblk) * BLK >= seq_lengths[0]).astype(jnp.int32)
    first, first_pull = jax.vjp(layer_norm, inputs, gain_first, shift_first)
    first_low = first.astype(jnp.bfloat16)
    projected = jnp.einsum("td,jdc->jtc", first_low, qkv_weight, preferred_element_type=jnp.float32)
    q_feat = rounded(feature(projected[0]))
    k_feat = rounded(feature(projected[1]))
    v_feat = rounded(projected[2])
    attended, attn_pull = jax.vjp(
        lambda a, b, c: linear_attention(a, b, c, stretch_seq), q_feat, k_feat, v_feat
    )
    attended_low = attended.astype(jnp.bfloat16)
    attn_part = jnp.dot(attended_low, out_weight, preferred_element_type=jnp.float32)
    middle = inputs + lax.psum(attn_part.astype(jnp.bfloat16), "tensor").astype(jnp.float32)
    second, second_pull = jax.vjp(layer_norm, middle, gain_second, shift_second)
    second_low = second.astype(jnp.bfloat16)
    hidden = jnp.dot(second_low, up_weight, preferred_element_type=jnp.float32) + up_bias
    active_low = jax.nn.silu(hidden).astype(jnp.bfloat16)
    ffn_part = jnp.dot(active_low, down_weight, preferred_element_type=jnp.float32)
    result = (
        middle + lax.psum(ffn_part.astype(jnp.bfloat16), "tensor").astype(jnp.float32)
    ).astype(jnp.bfloat16)
    grad_down = jnp.einsum("tf,td->fd", active_low, grad_low, preferred_element_type=jnp.float32)
    grad_active = jnp.einsum("td,fd->tf", grad_low, down_weight, preferred_element_type=jnp.float32)
    grad_hidden = (grad_active * silu_slope(hidden)).astype(jnp.bfloat16)
    grad_up = jnp.einsum("td,tf->df", second_low, grad_hidden, preferred_element_type=jnp.float32)
    grad_up_bias = jnp.sum(grad_hidden.astype(jnp.float32), axis=0)
    second_part = jnp.einsum(
        "tf,df->td", grad_hidden, up_weight, preferred_element_type=jnp.float32
    )
    grad_second = lax.psum(second_part.astype(jnp.bfloat16), "tensor").astype(jnp.float32)
    middle_norm, grad_gain_second, grad_shift_second = second_pull(grad_second)
    grad_middle = grad_low.astype(jnp.float32) + middle_norm
    middle_low = grad_middle.astype(jnp.bfloat16)
    grad_outproj = jnp.einsum(
        "tc,td->cd", attended_low, middle_low, preferred_element_type=jnp.float32
    )
    grad_attended = jnp.einsum(
        "td,cd->tc", middle_low, out_weight, preferred_element_type=jnp.float32
    )
    grad_qf, grad_kf, grad_vf = attn_pull(grad_attended)
    grad_proj = jnp.stack(
        [grad_qf * feature_slope(projected[0]), grad_kf * feature_slope(projected[1]), grad_vf]
    ).astype(jnp.bfloat16)
    grad_qkv = jnp.einsum("td,jtc->jdc", first_low, grad_proj, preferred_element_type=jnp.float32)
    first_part = jnp.einsum(
        "jtc,jdc->td", grad_proj, qkv_weight, preferred_element_type=jnp.float32
    )
    grad_first = lax.psum(first_part.astype(jnp.bfloat16), "tensor").astype(jnp.float32)
    input_norm, grad_gain_first, grad_shift_first = first_pull(grad_first)
    grad_inputs = (grad_middle + input_norm).astype(jnp.bfloat16)
    (
        grad_qkv,
        grad_outproj,
        grad_up,
        grad_down,
        grad_up_bias,
        grad_gain_first,
        grad_shift_first,
        grad_gain_second,
        grad_shift_second,
    ) = lax.psum(
        (
            grad_qkv,
            grad_outproj,
            grad_up,
            grad_down,
            grad_up_bias,
            grad_gain_first,
            grad_shift_first,
            grad_gain_second,
            grad_shift_second,
        ),
        "dp",
    )
    back = (
        result[local_pos].reshape(count, slot, -1),
        grad_inputs[local_pos].reshape(count, slot, -1),
    )
    got_out, got_input = (
        lax.all_to_all(back[0], "dp", split_axis=0, concat_axis=0, tiled=True),
        lax.all_to_all(back[1], "dp", split_axis=0, concat_axis=0, tiled=True),
    )
    undo = jnp.argsort(order)
    layer_out = got_out.reshape(rows, -1)[undo]
    grad_input = got_input.reshape(rows, -1)[undo]
    return (
        layer_out,
        grad_input,
        grad_qkv,
        grad_outproj,
        grad_up,
        grad_down,
        grad_gain_first,
        grad_shift_first,
        grad_gain_second,
        grad_shift_second,
        grad_up_bias,
    )


def solution(mesh):
    placed = (
        P("dp", None),
        P("dp"),
        P("dp"),
        P("dp", None),
        P(None, None, "tensor"),
        P("tensor", None),
        P(None, "tensor"),
        P("tensor", None),
        P(),
        P(),
        P(),
        P(),
        P("tensor"),
    )
    return jax.shard_map(
        per_device,
        mesh=mesh,
        in_specs=placed,
        out_specs=(
            P("dp", None),
            P("dp", None),
            P(None, None, "tensor"),
            P("tensor", None),
            P(None, "tensor"),
            P("tensor", None),
            P(),
            P(),
            P(),
            P(),
            P("tensor"),
        ),
        check_vma=False,
    )
```

profile of v0, /device:TPU:0, one launch (start us, length us, event | category | flops | bytes accessed | tf_op | source)
XLA Modules:
  0.0 935.9 jit_solution(12726560406458529215)
XLA Ops:
  7.2 5.9 sort.45
  13.1 20.6 %gather_fusion.1 = s32[2048]{0:T(1024)} fusion(s32[2048]{0:T(1024)S(1)} %copy-done.2, s32[2048]{0:T(1024)S(1)} %fusion.86), kind=kCustom, calls=%fused_computation.1 | custom fusion | bytes 24576 | tf_op jit(solution)/shard_map/gather | solution.py:81
  33.7 7.4 all-to-all-start.1
  41.0 9.2 gather_fusion
  50.2 6.0 all-to-all-start
  56.3 11.1 %gather_fusion.5 = bf16[2048,512]{1,0:T(8,128)(2,1)} fusion(bf16[2048,512]{1,0:T(8,128)(2,1)} %param.16, s32[2048]{0:T(1024)S(1)} %fusion.86), kind=kCustom, calls=%fused_computation.5 | custom fusion | bytes 4202496 | tf_op jit(solution)/shard_map/gather | solution.py:80
  67.5 5.0 sort.46
  72.5 24.8 %all-to-all-done = bf16[16,128,512]{2,1,0:T(8,128)(2,1)S(1)} async-done(((bf16[16,128,512]{2,1,0:T(8,128)(2,1)}), bf16[16,128,512]{2,1,0:T(8,128)(2,1)S(1)}, u32[]{:S(2)}, u32[]{:S(2)}) %all-to-all-start) | async-done | bytes 2097184 | tf_op jit(solution)/shard_map/all_to_all | solution.py:84
  97.4 11.3 %all-to-all-start.3 = ((bf16[16,128,512]{2,1,0:T(8,128)(2,1)}), bf16[16,128,512]{2,1,0:T(8,128)(2,1)}, u32[]{:S(2)}, u32[]{:S(2)}) async-start(bf16[16,128,512]{2,1,0:T(8,128)(2,1)} %bitcast.114), calls=%async_computation.3 | async-start | bytes 4194304 | tf_op jit(solution)/shard_map/all_to_all | solution.py:85
  108.9 9.5 %gather_fusion.2 = bf16[2048,512]{1,0:T(8,128)(2,1)S(1)} fusion(bf16[2048,512]{1,0:T(8,128)(2,1)} %bitcast.113, s32[2048]{0:T(1024)S(1)} %fusion.87), kind=kCustom, calls=%fused_computation.2 | custom fusion | bytes 4202496 | tf_op jit(solution)/shard_map/gather | solution.py:90
  127.4 4.4 reshape.268
  131.8 4.4 reshape.269
  140.7 4.3 copy.119
  145.1 3.1 fusion.52
  148.5 4.9 fusion.27
  158.4 7.2 fusion.29
  165.7 4.8 fusion.23
  173.2 3.4 convert_element_type.111
  178.8 11.3 %gather_fusion.6 = bf16[2048,512]{1,0:T(8,128)(2,1)} fusion(bf16[2048,512]{1,0:T(8,128)(2,1)} %bitcast.22, s32[2048]{0:T(1024)S(1)} %fusion.87), kind=kCustom, calls=%fused_computation.6 | custom fusion | bytes 4202496 | tf_op jit(solution)/shard_map/gather | solution.py:91
  190.1 53.0 %all-reduce.8.cloned.1.call-done = bf16[2048,512]{1,0:T(8,128)(2,1)} async-done(((bf16[2048,512]{1,0:T(8,128)(2,1)}), bf16[2048,512]{1,0:T(8,128)(2,1)}) %all-reduce.8.cloned.1.call-update) | async-done | bytes 2097168 | tf_op jit(solution)/shard_map/psum | solution.py:105
  246.6 5.7 multiply_convert_fusion.1
  252.3 5.1 convert_reduce_fusion
  259.4 3.8 convolution_convert_fusion
  263.4 6.2 convolution_convert_fusion.1
  269.5 56.8 %all-reduce.10.cloned.1.call-done = bf16[2048,512]{1,0:T(8,128)(2,1)} async-done(((bf16[2048,512]{1,0:T(8,128)(2,1)}), bf16[2048,512]{1,0:T(8,128)(2,1)}) %all-reduce.10.cloned.1.call-update) | async-done | bytes 2097168 | tf_op jit(solution)/shard_map/psum | solution.py:122
  326.4 4.1 fusion.13
  338.5 5.1 reshape.276
  343.6 15.5 %fusion.15 = f32[32,4,64,64]{3,2,1,0:T(8,128)} fusion(f32[32,4,64,64]{2,3,1,0:T(8,128)} %copy-done.30, f32[64,64]{0,1:T(8,128)S(1)} %fusion.79, f32[32,64,4,64]{1,0,3,2:T(8,128)} %reshape.276, f32[32,64,4]{1,2,0:T(4,128)S(1)} %copy-done.53), kind=kOutput, calls=%fused_computation.41 | convolution fusion | flops 403701760 | bytes 6340608 | tf_op jit(solution)/shard_map/transpose(jvp(chij,cjhf->cihf))/dot_general | solution.py:52
  359.1 13.6 %fusion.21 = f32[32,4,64,64]{2,3,1,0:T(8,128)} fusion(f32[32,4,64,64]{3,0,2,1:T(8,128)S(1)} %copy-done.22, f32[32,64,4,64]{1,0,3,2:T(8,128)S(1)} %copy-done.23, f32[32,64,4]{1,2,0:T(4,128)S(1)} %copy-done.53), kind=kOutput, calls=%fused_computation.47 | convolution fusion | flops 403177472 | bytes 6324224 | tf_op jit(solution)/shard_map/transpose(jvp(cihe,chef->cihf))/dot_general | solution.py:51
  372.7 6.8 fusion.17
  379.5 7.5 fusion.19
  387.1 3.4 fusion.24
  392.5 6.8 fusion.25
  399.3 5.7 copy.126
  405.0 5.6 fusion.32
  410.9 4.5 fusion.51
  418.2 5.6 copy.124
  423.9 5.4 reshape.278
  429.3 4.2 copy.128
  433.5 4.3 reshape.279
  437.9 9.9 %add_bitcast_fusion = f32[32,64,4,64]{1,3,2,0:T(8,128)} fusion(f32[32,4,64,64]{2,3,1,0:T(8,128)} %fusion.21, f32[32,4,64,64]{2,3,1,0:T(8,128)} %fusion.19, f32[32,4,64]{2,1,0:T(4,128)S(1)} %copy.105, f32[32,4,64]{2,1,0:T(4,128)S(1)} %get-tuple-element.83, f32[64,64]{0,1:T(8,128)S(1)} %fusion.79, bf16[32,64,4,64]{3,2,1,0:T(4,128)(2,1)} %reshape.267), kind=kOutput, calls=%fused_computation.59 | convolution fusion | flops 405274624 | bytes 7421952 | tf_op jit(solution)/shard_map/transpose(jvp(cihe,cjhe->chij))/dot_general | solution.py:48
  447.7 5.3 copy.116
  453.0 5.5 reshape.277
  458.6 4.6 multiply_convert_fusion.3
  464.5 3.2 bitcast_convert_fusion
  468.5 107.7 %all-reduce.14.cloned.1.call-done = (bf16[2048,512]{1,0:T(8,128)(2,1)}, bf16[2048,512]{1,0:T(8,128)(2,1)}) async-done(((bf16[2048,512]{1,0:T(8,128)(2,1)}, bf16[2048,512]{1,0:T(8,128)(2,1)}), (bf16[2048,512]{1,0:T(8,128)(2,1)}, bf16[2048,512]{1,0:T(8,128)(2,1)})) %all-reduce.14.cloned.1.call-update) | async-done | bytes 4194320 | tf_op jit(solution)/shard_map/psum | solution.py:112
  576.2 3.4 convert_reduce_fusion.1
  579.6 3.6 fusion.14
  583.3 5.8 add_convert_fusion
  589.1 11.1 %gather_fusion.7 = bf16[2048,512]{1,0:T(8,128)(2,1)} fusion(bf16[2048,512]{1,0:T(8,128)(2,1)} %get-tuple-element.80, s32[2048]{0:T(1024)S(1)} %broadcast_clamp_fusion), kind=kCustom, calls=%fused_computation.7 | custom fusion | bytes 4202496 | tf_op jit(solution)/shard_map/gather | solution.py:169
  600.2 5.9 all-to-all-start.4
  606.2 6.7 fusion.104
  612.9 4.0 fusion.98
  616.9 11.1 %gather_fusion.3 = bf16[2048,512]{1,0:T(8,128)(2,1)} fusion(bf16[2048,512]{1,0:T(8,128)(2,1)} %get-tuple-element.81, s32[2048]{0:T(1024)S(1)} %broadcast_clamp_fusion), kind=kCustom, calls=%fused_computation.3 | custom fusion | bytes 4202496 | tf_op jit(solution)/shard_map/gather | solution.py:168
  628.0 19.3 %all-to-all-done.4 = bf16[16,128,512]{2,1,0:T(8,128)(2,1)} async-done(((bf16[16,128,512]{2,1,0:T(8,128)(2,1)}), bf16[16,128,512]{2,1,0:T(8,128)(2,1)}, u32[]{:S(2)}, u32[]{:S(2)}) %all-to-all-start.4) | async-done | bytes 2097184 | tf_op jit(solution)/shard_map/all_to_all | solution.py:173
  647.3 11.3 %all-to-all-start.2 = ((bf16[16,128,512]{2,1,0:T(8,128)(2,1)}), bf16[16,128,512]{2,1,0:T(8,128)(2,1)}, u32[]{:S(2)}, u32[]{:S(2)}) async-start(bf16[16,128,512]{2,1,0:T(8,128)(2,1)} %bitcast.115), calls=%async_computation.2 | async-start | bytes 4194304 | tf_op jit(solution)/shard_map/all_to_all | solution.py:172
  658.6 3.1 fusion.103
  661.7 5.1 convolution_bitcast_fusion.1
  667.6 5.0 sort.47
  672.6 164.9 %all-reduce.12.cloned.1.call-done = (f32[3,512,256]{1,2,0:T(8,128)}, f32[256,512]{1,0:T(8,128)}, f32[512,1024]{1,0:T(8,128)}, f32[1024,512]{1,0:T(8,128)}) async-done(((f32[3,512,256]{1,2,0:T(8,128)}, f32[256,512]{1,0:T(8,128)}, f32[512,1024]{1,0:T(8,128)}, f32[1024,512]{1,0:T(8,128)}), (f32[3,512,256]{1,2,0:T(8,128)}, f32[256,512]{1,0:T(8,128)}, f32[512,1024]{1,0:T(8,128)}, ...) | async-done | bytes 6291472 | tf_op jit(solution)/shard_map/psum | solution.py:153
  840.6 60.4 %all-reduce = (f32[512]{0:T(512)}, f32[512]{0:T(512)}, f32[512]{0:T(512)}, f32[512]{0:T(512)}, f32[1024]{0:T(1024)}) all-reduce(f32[512]{0:T(512)S(1)} %get-tuple-element.52, f32[512]{0:T(512)S(1)} %get-tuple-element.55, f32[512]{0:T(512)S(1)} %get-tuple-element.50, ...), channel_id=1, replica_groups=mesh['dp'=16,'tensor'=2] {'dp'}, use_global_device_ids=true, to_apply=%region_23.24 | all-reduce | flops 3072 | bytes 24576 | tf_op jit(solution)/shard_map/psum | solution.py:153
  901.0 11.1 %gather_fusion.8 = bf16[2048,512]{1,0:T(8,128)(2,1)} fusion(bf16[2048,512]{1,0:T(8,128)(2,1)} %bitcast.37, s32[2048]{0:T(1024)S(1)} %fusion.88), kind=kCustom, calls=%fused_computation.8 | custom fusion | bytes 4202496 | tf_op jit(solution)/shard_map/gather | solution.py:177
  912.1 11.2 %gather_fusion.4 = bf16[2048,512]{1,0:T(8,128)(2,1)} fusion(bf16[2048,512]{1,0:T(8,128)(2,1)} %bitcast.20, s32[2048]{0:T(1024)S(1)} %fusion.88), kind=kCustom, calls=%fused_computation.4 | custom fusion | bytes 4202496 | tf_op jit(solution)/shard_map/gather | solution.py:176
  924.1 3.7 copy.220
  (197 shorter events, 50.5 us)
Async XLA Ops:
  7.2 33.9 %copy-start = (bf16[2048,512]{1,0:T(8,128)(2,1)S(1)}, bf16[2048,512]{1,0:T(8,128)(2,1)}, u32[]{:S(2)}) copy-start(bf16[2048,512]{1,0:T(8,128)(2,1)} %param.13) | copy-start | bytes 6291460
  7.2 5.9 copy-start.2
  13.1 20.6 %copy-start.54 = (s32[2048]{0:T(1024)}, s32[2048]{0:T(1024)S(1)}, u32[]{:S(2)}) copy-start(s32[2048]{0:T(1024)S(1)} %get-tuple-element.14) | copy-start | bytes 24580
  33.7 16.6 %all-to-all-start.1 = ((s32[16,1,128]{2,1,0:T(1,128)}), s32[16,1,128]{2,1,0:T(1,128)S(1)}, u32[]{:S(2)}, u32[]{:S(2)}) async-start(s32[16,1,128]{2,1,0:T(1,128)} %bitcast.2), calls=%async_computation.1 | async-start | bytes 16384 | tf_op jit(solution)/shard_map/all_to_all | solution.py:86
  50.2 17.2 %copy-start.50 = (s32[16,1,128]{2,1,0:T(1,128)}, s32[16,1,128]{2,1,0:T(1,128)S(1)}, u32[]{:S(2)}) copy-start(s32[16,1,128]{2,1,0:T(1,128)S(1)} %all-to-all-done.1) | copy-start | bytes 24580
  50.2 47.1 %all-to-all-start = ((bf16[16,128,512]{2,1,0:T(8,128)(2,1)}), bf16[16,128,512]{2,1,0:T(8,128)(2,1)S(1)}, u32[]{:S(2)}, u32[]{:S(2)}) async-start(bf16[16,128,512]{2,1,0:T(8,128)(2,1)} %bitcast.116), calls=%async_computation | async-start | bytes 4194304 | tf_op jit(solution)/shard_map/all_to_all | solution.py:84
  56.3 11.1 %copy-start.67 = (s32[2]{0:T(128)S(1)}, s32[2]{0:T(128)}, u32[]{:S(2)}) copy-start(s32[2]{0:T(128)} %param.14) | copy-start | bytes 28
  97.4 11.5 %copy-start.3 = (bf16[16,128,512]{2,1,0:T(8,128)(2,1)}, bf16[16,128,512]{2,1,0:T(8,128)(2,1)S(1)}, u32[]{:S(2)}) copy-start(bf16[16,128,512]{2,1,0:T(8,128)(2,1)S(1)} %all-to-all-done) | copy-start | bytes 6291460
  97.4 81.4 %all-to-all-start.3 = ((bf16[16,128,512]{2,1,0:T(8,128)(2,1)}), bf16[16,128,512]{2,1,0:T(8,128)(2,1)}, u32[]{:S(2)}, u32[]{:S(2)}) async-start(bf16[16,128,512]{2,1,0:T(8,128)(2,1)} %bitcast.114), calls=%async_computation.3 | async-start | bytes 4194304 | tf_op jit(solution)/shard_map/all_to_all | solution.py:85
  108.6 134.5 %all-reduce.8.cloned.1.call-start = ((), (), s32[]{:S(2)}) async-start(), calls=%async_computation.5 | async-start | bytes 4194304 | tf_op jit(solution)/shard_map/psum | solution.py:105
  118.7 3.3 copy-start.44
  148.5 6.3 copy-start.42
  148.5 5.0 copy-start.4
  148.5 5.0 copy-start.10
  153.5 4.9 copy-start.21
  153.5 3.2 copy-start.34
  154.8 10.9 %copy-start.30 = (f32[32,4,64,64]{2,3,1,0:T(8,128)}, f32[32,4,64,64]{2,3,1,0:T(8,128)S(1)}, u32[]{:S(2)}) copy-start(f32[32,4,64,64]{2,3,1,0:T(8,128)S(1)} %get-tuple-element.85) | copy-start | bytes 6291460
  158.4 7.3 copy-start.52
  158.4 7.3 copy-start.18
  170.5 6.1 copy-start.40
  176.6 13.5 %copy-start.26 = (bf16[2048,256]{0,1:T(8,128)(2,1)}, bf16[2048,256]{0,1:T(8,128)(2,1)S(1)}, u32[]{:S(2)}) copy-start(bf16[2048,256]{0,1:T(8,128)(2,1)S(1)} %convert_element_type.111) | copy-start | bytes 3145732
  178.8 147.6 %all-reduce.10.cloned.1.call-start = ((), (), s32[]{:S(2)}) async-start(), calls=%async_computation.6 | async-start | bytes 4194304 | tf_op jit(solution)/shard_map/psum | solution.py:122
  190.1 56.5 %copy-start.58 = (f32[512]{0:T(512)S(1)}, f32[512]{0:T(512)}, u32[]{:S(2)}) copy-start(f32[512]{0:T(512)} %param.23) | copy-start | bytes 6148
  190.1 56.5 %copy-start.63 = (f32[1024]{0:T(1024)S(1)}, f32[1024]{0:T(1024)}, u32[]{:S(2)}) copy-start(f32[1024]{0:T(1024)} %param.25) | copy-start | bytes 12292
  190.1 56.5 %copy-start.64 = (f32[512]{0:T(512)S(1)}, f32[512]{0:T(512)}, u32[]{:S(2)}) copy-start(f32[512]{0:T(512)} %param.24) | copy-start | bytes 6148
  243.1 3.5 copy-start.59
  246.6 5.7 copy-start.15
  246.6 5.7 copy-start.60
  259.4 3.9 copy-start.43
  263.3 312.9 %all-reduce.14.cloned.1.call-start = ((), (), s32[]{:S(2)}) async-start(), calls=%async_computation.8 | async-start | bytes 8388608 | tf_op jit(solution)/shard_map/psum | solution.py:112
  326.4 4.1 copy-start.7
  326.4 4.1 copy-start.28
  338.4 5.1 copy-start.53
  343.6 15.5 %copy-start.22 = (f32[32,4,64,64]{3,0,2,1:T(8,128)S(1)}, f32[32,4,64,64]{3,0,2,1:T(8,128)}, u32[]{:S(2)}) copy-start(f32[32,4,64,64]{3,0,2,1:T(8,128)} %copy-done.21) | copy-start | bytes 6291460
  343.6 15.5 %copy-start.23 = (f32[32,64,4,64]{1,0,3,2:T(8,128)S(1)}, f32[32,64,4,64]{1,0,3,2:T(8,128)}, u32[]{:S(2)}) copy-start(f32[32,64,4,64]{1,0,3,2:T(8,128)} %reshape.276) | copy-start | bytes 6291460
  359.1 13.6 %copy-start.35 = (bf16[32,64,4,64]{1,3,2,0:T(8,128)(2,1)S(1)}, bf16[32,64,4,64]{1,3,2,0:T(8,128)(2,1)}, u32[]{:S(2)}) copy-start(bf16[32,64,4,64]{1,3,2,0:T(8,128)(2,1)} %copy.119) | copy-start | bytes 3145732
  372.7 6.8 copy-start.19
  379.5 7.5 copy-start.31
  387.1 3.4 copy-start.11
  405.0 5.7 copy-start.5
  405.0 5.7 copy-start.12
  405.0 5.9 copy-start.29
  410.9 4.5 copy-start.20
  453.0 5.6 copy-start.32
  453.0 5.6 copy-start.33
  458.6 6.0 copy-start.37
  458.6 6.0 copy-start.62
  467.7 108.4 %copy-start.45 = (f32[2048]{0:T(1024)S(1)}, f32[2048]{0:T(1024)}, u32[]{:S(2)}) copy-start(f32[2048]{0:T(1024)} %copy-done.44) | copy-start | bytes 24580
  467.7 108.4 %copy-start.57 = (f32[512]{0:T(512)S(1)}, f32[512]{0:T(512)}, u32[]{:S(2)}) copy-start(f32[512]{0:T(512)} %param.21) | copy-start | bytes 6148
  467.7 111.9 %copy-start.49 = (f32[2048]{0:T(1024)S(1)}, f32[2048]{0:T(1024)}, u32[]{:S(2)}) copy-start(f32[2048]{0:T(1024)} %copy-done.48) | copy-start | bytes 24580
  467.7 111.9 %copy-start.47 = (f32[2048]{0:T(1024)S(1)}, f32[2048]{0:T(1024)}, u32[]{:S(2)}) copy-start(f32[2048]{0:T(1024)} %copy-done.46) | copy-start | bytes 24580
  576.2 7.1 copy-start.8
  576.2 7.1 copy-start.14
  576.2 7.1 copy-start.17
  600.2 47.1 %all-to-all-start.4 = ((bf16[16,128,512]{2,1,0:T(8,128)(2,1)}), bf16[16,128,512]{2,1,0:T(8,128)(2,1)}, u32[]{:S(2)}, u32[]{:S(2)}) async-start(bf16[16,128,512]{2,1,0:T(8,128)(2,1)} %bitcast.117), calls=%async_computation.4 | async-start | bytes 4194304 | tf_op jit(solution)/shard_map/all_to_all | solution.py:173
  606.2 6.7 copy-start.9
  606.2 6.7 copy-start.69
  628.0 30.6 %copy-start.27 = (bf16[2048,256]{0,1:T(8,128)(2,1)S(1)}, bf16[2048,256]{0,1:T(8,128)(2,1)}, u32[]{:S(2)}) copy-start(bf16[2048,256]{0,1:T(8,128)(2,1)} %copy-done.26) | copy-start | bytes 3145732
  628.0 33.7 %copy-start.66 = (f32[512]{0:T(512)S(1)}, f32[512]{0:T(512)}, u32[]{:S(2)}) copy-start(f32[512]{0:T(512)} %param.22) | copy-start | bytes 6148
  647.3 264.8 %all-to-all-start.2 = ((bf16[16,128,512]{2,1,0:T(8,128)(2,1)}), bf16[16,128,512]{2,1,0:T(8,128)(2,1)}, u32[]{:S(2)}, u32[]{:S(2)}) async-start(bf16[16,128,512]{2,1,0:T(8,128)(2,1)} %bitcast.115), calls=%async_computation.2 | async-start | bytes 4194304 | tf_op jit(solution)/shard_map/all_to_all | solution.py:172
  658.6 179.0 %all-reduce.12.cloned.1.call-start = ((), (), s32[]{:S(2)}) async-start(), calls=%async_computation.7 | async-start | bytes 12582912 | tf_op jit(solution)/shard_map/psum | solution.py:153
  912.1 11.2 %copy-start.41 = (f32[256,512]{1,0:T(8,128)S(1)}, f32[256,512]{1,0:T(8,128)}, u32[]{:S(2)}) copy-start(f32[256,512]{1,0:T(8,128)} %get-tuple-element.95) | copy-start | bytes 1572868
  923.3 4.5 copy-start.36
  923.3 5.9 copy-start.1
  (15 other events, 25.7 us)
Sparse Core Ops, SparseCore 0:
  178.9 64.1 all-reduce.7
  263.4 62.9 all-reduce.9
  467.9 108.2 all-reduce.13
  667.0 170.4 all-reduce.11
where the time goes:
time: 941 us; the launch traced here: 936 us
  waiting for transfers between devices  427 us (45%)
  local copies, waits for them, and re-layouts  190 us (20%)
  matrix products  148 us (16%)
  blocking collectives  60.4 us (6%)
  other arithmetic  54 us (6%)
  starting transfers between devices  42.2 us (4%)
  between operations  15.1 us (2%)
    psum x1, waiting for transfers between devices, per_device(): lax.psum((grad_qkv, grad_outproj, grad_up, grad_down, grad_up_bias, grad_...  165 us
    psum x1, waiting for transfers between devices, per_device(): lax.psum(ffn_part.astype(jnp.bfloat16), 'tensor').astype(jnp.float32)  108 us
    psum x1, blocking collectives, per_device(): lax.psum((grad_qkv, grad_outproj, grad_up, grad_down, grad_up_bias, grad_...  60.4 us
    psum x1, waiting for transfers between devices, per_device(): lax.psum(second_part.astype(jnp.bfloat16), 'tensor').astype(jnp.float32)  56.8 us
    psum x1, waiting for transfers between devices, per_device(): lax.psum(attn_part.astype(jnp.bfloat16), 'tensor').astype(jnp.float32)  53 us
    dot_general x3, matrix products, linear_attention(): jnp.einsum('chij,cjhf->cihf', scores, values, precision=best)  27.8 us
    dot_general x3, matrix products, linear_attention(): numer = jnp.einsum('cihe,chef->cihf', query, state, precision=best)  27.6 us
    all_to_all x1, waiting for transfers between devices, per_device(): lax.all_to_all(sent[0], 'dp', split_axis=0, concat_axis=0, tiled=True)  24.8 us
  transfers between devices with their start and end apart: 9, of which 6 were waited for; matrix products, arithmetic and copies ran while one was open for 17% of the time, Pallas kernels for 0%

commit v1 on v0

v1 whole, which is shorter than its diff:
```python
import functools

import jax
import jax.numpy as jnp
from jax import lax
from jax.experimental import pallas as pl
from jax.experimental.pallas import tpu as pltpu
from jax.sharding import PartitionSpec as P

HD = 64
BLK = 64
TILE = 256
HEADER = 8
EPS = 1e-05
BF16 = jnp.bfloat16
F32 = jnp.float32
VMEM_LIMIT = 56 * 1024 * 1024


def dot(a, b):
    return jnp.dot(a, b, preferred_element_type=F32)


def dot_t(a, b):
    return lax.dot_general(a, b, (((1,), (1,)), ((), ())), preferred_element_type=F32)


def iota(shape, dim):
    return lax.broadcasted_iota(jnp.int32, shape, dim)


def one_hot(match):
    return jnp.where(match, 1.0, 0.0).astype(BF16)


def call(body, outs, scratch=(), in_specs=None, flops=0, moved=0, trans=0, limit=VMEM_LIMIT):
    return pl.pallas_call(
        body,
        out_shape=outs,
        in_specs=in_specs,
        scratch_shapes=list(scratch),
        compiler_params=pltpu.CompilerParams(vmem_limit_bytes=limit),
        cost_estimate=pl.CostEstimate(flops=flops, bytes_accessed=moved, transcendentals=trans),
    )


def shaped(shape, kind):
    return jax.ShapeDtypeStruct(shape, kind)


SMEM = pl.BlockSpec(memory_space=pltpu.SMEM)
VMEM = pl.BlockSpec(memory_space=pltpu.VMEM)


def send_tokens_body(ids_ref, slot_ref, tok_ref, out_ref, place_ref):
    own_plane = ids_ref[1]
    rows = tok_ref.shape[0]
    count, slot = out_ref.shape[0], out_ref.shape[1] - HEADER
    half = out_ref.shape[2]
    slots = slot_ref[...]
    block = slots // rows
    local = slots - block * rows
    member = one_hot(iota((count, rows), 0) == block)
    before = one_hot(iota((TILE, TILE), 0) < iota((TILE, TILE), 1))
    carry = jnp.zeros((count, 1), F32)
    ranks = []
    for at in range(0, rows, TILE):
        seg = member[:, at : at + TILE]
        inside = dot(seg, before) + carry
        segf = seg.astype(F32)
        ranks.append(jnp.sum(segf * inside, axis=0, keepdims=True))
        carry = carry + jnp.sum(segf, axis=1, keepdims=True)
    rank = jnp.concatenate(ranks, axis=1).astype(jnp.int32)
    pair = block // 2
    place = pair * slot + rank + jnp.where(block - 2 * pair == own_plane, 0, rows // 2)
    place_ref[...] = place
    high = local // 128
    low = local - high * 128
    line = iota((16, rows), 0)
    marks = jnp.where(line == 0, high, jnp.where(line == 1, low, 0)).astype(F32).astype(BF16)
    per = TILE // slot

    def step(t, _):
        pick = one_hot(iota((TILE, rows), 0) + t * TILE == place)
        moved = dot(pick, tok_ref[...]).astype(BF16)
        head = dot_t(marks, pick)[:HEADER].astype(BF16)
        for j in range(per):
            for side in range(2):
                to = 2 * (t * per + j) + side
                out_ref[to, 0:slot, :] = moved[
                    j * slot : (j + 1) * slot, side * half : (side + 1) * half
                ]
                out_ref[to, slot : slot + HEADER, :] = head
        return 0

    lax.fori_loop(0, rows // 2 // TILE, step, 0)


def send_grads_body(place_ref, tok_ref, out_ref):
    rows = tok_ref.shape[0]
    slot, half = out_ref.shape[1], out_ref.shape[2]
    per = TILE // slot
    place = place_ref[...]

    def step(t, _):
        pick = one_hot(iota((TILE, rows), 0) + t * TILE == place)
        moved = dot(pick, tok_ref[...]).astype(BF16)
        for j in range(per):
            for side in range(2):
                out_ref[2 * (t * per + j) + side] = moved[
                    j * slot : (j + 1) * slot, side * half : (side + 1) * half
                ]
        return 0

    lax.fori_loop(0, rows // 2 // TILE, step, 0)


def received(core, pick, mine, other):
    a = dot(pick, mine)
    b = dot(pick, other)
    first = core == 0
    return jnp.concatenate([jnp.where(first, a, b), jnp.where(first, b, a)], axis=1)


def norm_parts(value):
    mean = jnp.mean(value, axis=-1, keepdims=True)
    cent = value - mean
    var = jnp.mean(cent * cent, axis=-1, keepdims=True)
    inv = lax.rsqrt(var + EPS)
    return cent * inv, inv


def norm_back(grad, xhat, inv, gain):
    e = grad * gain
    m1 = jnp.mean(e, axis=-1, keepdims=True)
    m2 = jnp.mean(e * xhat, axis=-1, keepdims=True)
    return inv * (e - m1 - xhat * m2)


def feature(value):
    return jnp.where(value > 0, value + 1.0, jnp.exp(jnp.minimum(value, 0.0)))


def head_mask(kind):
    n = 4 * HD
    return (iota((n, n), 0) // HD == iota((n, n), 1) // HD).astype(F32).astype(kind)


def spread(x, mask):
    return jnp.concatenate([x, x, x, x], axis=0) * mask


def attend_body(
    ids_ref, spos_ref, mine_ref, other_ref, wown_ref, wa_ref, wb_ref, oown_ref, oa_ref, ob_ref,
    gain_ref, shift_ref,
    x_ref, h1_ref, qkv_ref, o_ref, rden_ref, s_ref, z_ref, m_ref,
    wg_ref, og_ref, state_ref, zsum_ref,
):
    core = ids_ref[0]
    count, slot, half = mine_ref.shape[0], mine_ref.shape[1] - HEADER, mine_ref.shape[2]
    rows = count * slot
    seq = rows // 2
    width = 4 * HD
    for j in range(3):
        wg_ref[j, :, 0 : width // 2] = wa_ref[j]
        wg_ref[j, :, width // 2 : width] = wb_ref[j]
    og_ref[0 : width // 2, :] = oa_ref[...]
    og_ref[width // 2 : width, :] = ob_ref[...]
    spos = spos_ref[...]
    gain, shift = gain_ref[...], shift_ref[...]

    def project(t, _):
        at = pl.multiple_of(t * TILE, TILE)
        pick = one_hot(iota((TILE, rows), 0) + core * seq + t * TILE == spos)
        mine = mine_ref[:, 0:slot, :].reshape(rows, half)
        other = other_ref[:, 0:slot, :].reshape(rows, half)
        x = received(core, pick, mine, other)
        x_ref[pl.ds(at, TILE), :] = x.astype(BF16)
        xhat, _inv = norm_parts(x)
        h1 = (xhat * gain + shift).astype(BF16)
        h1_ref[pl.ds(at, TILE), :] = h1
        for g in range(2):
            for j in range(3):
                w = wown_ref[j] if g == 0 else wg_ref[j]
                u = dot(h1, w)
                if j < 2:
                    u = feature(u)
                qkv_ref[j, g, pl.ds(at, TILE), :] = u.astype(BF16)
        return 0

    lax.fori_loop(0, seq // TILE, project, 0)

    state_ref[...] = jnp.zeros_like(state_ref)
    zsum_ref[...] = jnp.zeros_like(zsum_ref)
    maskf = head_mask(F32)
    mask = maskf.astype(BF16)
    lower = iota((BLK, width), 1) % BLK <= iota((BLK, width), 0)

    def chunk(c, _):
        at = pl.multiple_of(c * BLK, BLK)
        for g in range(2):
            q = qkv_ref[0, g, pl.ds(at, BLK), :]
            k = qkv_ref[1, g, pl.ds(at, BLK), :]
            v = qkv_ref[2, g, pl.ds(at, BLK), :]
            state = state_ref[g]
            low = state.astype(BF16)
            s_ref[g, c] = low
            z = zsum_ref[g]
            z_ref[g, c] = z
            scores = jnp.where(lower, dot_t(q, spread(k, mask)), 0.0)
            num = dot(q, low) + dot(scores.astype(BF16), spread(v, mask))
            den = dot((scores + q.astype(F32) * z[0:1]).astype(BF16), mask) + 1e-06
            rden = 1.0 / den
            rden_ref[g, pl.ds(at, BLK), :] = rden
            o_ref[g, pl.ds(at, BLK), :] = (num * rden).astype(BF16)
            state_ref[g] = state + dot(k.T, v) * maskf
            zsum_ref[g] = z + jnp.sum(k.astype(F32), axis=0, keepdims=True)
        return 0

    lax.fori_loop(0, seq // BLK, chunk, 0, unroll=2)

    def output(t, _):
        at = pl.multiple_of(t * TILE, TILE)
        att = dot(o_ref[0, pl.ds(at, TILE), :], oown_ref[...])
        att = att + dot(o_ref[1, pl.ds(at, TILE), :], og_ref[...])
        m_ref[pl.ds(at, TILE), :] = x_ref[pl.ds(at, TILE), :].astype(F32) + att
        return 0

    lax.fori_loop(0, seq // TILE, output, 0)


def ffn_body(
    ids_ref, spos_ref, mine_ref, other_ref, m_ref, uown_ref, ua_ref, ub_ref,
    down_ref, da_ref, db_ref, bias_ref, gain_ref, shift_ref,
    keep_ref, send_ref, dm_ref, grad_ref, vec_ref, bvec_ref,
    gpt_ref, h2t_ref, rl_ref, du_ref,
):
    core = ids_ref[0]
    count, slot, half = mine_ref.shape
    rows = count * slot
    seq = rows // 2
    unit = ua_ref.shape[1]
    spos = spos_ref[...]
    gain, shift = gain_ref[...], shift_ref[...]
    vec_ref[...] = jnp.zeros_like(vec_ref)
    bvec_ref[...] = jnp.zeros_like(bvec_ref)

    def up_piece(j):
        if j < 2:
            return uown_ref[:, j * unit : (j + 1) * unit]
        return ua_ref[...] if j == 2 else ub_ref[...]

    def down_piece(j):
        if j < 2:
            return down_ref[j * unit : (j + 1) * unit, :]
        return da_ref[...] if j == 2 else db_ref[...]

    def tile(t, _):
        at = pl.multiple_of(t * TILE, TILE)
        pick = one_hot(iota((TILE, rows), 0) + core * seq + t * TILE == spos)
        gpf = received(core, pick, mine_ref[...].reshape(rows, half), other_ref[...].reshape(rows, half))
        gp = gpf.astype(BF16)
        m = m_ref[pl.ds(at, TILE), :]
        xhat, inv = norm_parts(m)
        h2 = (xhat * gain + shift).astype(BF16)
        gpt_ref[:, pl.ds(at, TILE)] = gp.T
        h2t_ref[:, pl.ds(at, TILE)] = h2.T
        f = jnp.zeros((TILE, m.shape[1]), F32)
        dh2 = jnp.zeros((TILE, m.shape[1]), F32)
        for j in range(4):
            up, down = up_piece(j), down_piece(j)
            u = dot(h2, up) + bias_ref[j : j + 1, :]
            sig = jax.nn.sigmoid(u)
            rl = (u * sig).astype(BF16)
            rl_ref[j, pl.ds(at, TILE), :] = rl
            f = f + dot(rl, down)
            du = dot_t(gp, down) * (sig * (1.0 + u * (1.0 - sig)))
            dul = du.astype(BF16)
            du_ref[j, pl.ds(at, TILE), :] = dul
            bvec_ref[j : j + 1, :] += jnp.sum(dul.astype(F32), axis=0, keepdims=True)
            dh2 = dh2 + dot_t(dul, up)
        out = (m + f).astype(BF16)
        left, right = out[:, :half], out[:, half:]
        first = core == 0
        keep_ref[pl.ds(at, TILE), :] = jnp.where(first, left, right)
        send_ref[pl.ds(at, TILE), :] = jnp.where(first, right, left)
        vec_ref[0:1, :] += jnp.sum(dh2 * xhat, axis=0, keepdims=True)
        vec_ref[1:2, :] += jnp.sum(dh2, axis=0, keepdims=True)
        dm_ref[pl.ds(at, TILE), :] = gpf + norm_back(dh2, xhat, inv, gain)
        return 0

    lax.fori_loop(0, seq // TILE, tile, 0)

    for j in range(4):
        where = (j ^ core) if j < 2 else j - 2
        side = 0 if j < 2 else 1
        grad_ref[where, side, 0] = dot(h2t_ref[...], du_ref[j]).astype(BF16)
        grad_ref[where, side, 1] = dot(gpt_ref[...], rl_ref[j]).astype(BF16)


def attend_back_body(
    ids_ref, dm_ref, oown_ref, oa_ref, ob_ref, qkv_ref, o_ref, rden_ref, s_ref, z_ref,
    h1_ref, x_ref, wown_ref, wa_ref, wb_ref, gain_ref,
    keep_ref, send_ref, grad_ref, vec_ref,
    wg_ref, og_ref, dmt_ref, h1t_ref, dn_ref, w_ref, dr_ref, state_ref, zsum_ref,
):
    core = ids_ref[0]
    seq, d = dm_ref.shape
    width = 4 * HD
    part = width // 2
    half = keep_ref.shape[1]
    for j in range(3):
        wg_ref[j, :, 0:part] = wa_ref[j]
        wg_ref[j, :, part:width] = wb_ref[j]
    og_ref[0:part, :] = oa_ref[...]
    og_ref[part:width, :] = ob_ref[...]
    vec_ref[...] = jnp.zeros_like(vec_ref)

    def start(t, _):
        at = pl.multiple_of(t * TILE, TILE)
        dml = dm_ref[pl.ds(at, TILE), :].astype(BF16)
        dmt_ref[:, pl.ds(at, TILE)] = dml.T
        h1t_ref[:, pl.ds(at, TILE)] = h1_ref[pl.ds(at, TILE), :].T
        for g in range(2):
            do = dot_t(dml, oown_ref[...] if g == 0 else og_ref[...])
            dn = do * rden_ref[g, pl.ds(at, TILE), :]
            dn_ref[g, pl.ds(at, TILE), :] = dn.astype(BF16)
            w_ref[g, pl.ds(at, TILE), :] = (
                -dn * o_ref[g, pl.ds(at, TILE), :].astype(F32)
            ).astype(BF16)
        return 0

    lax.fori_loop(0, seq // TILE, start, 0)

    state_ref[...] = jnp.zeros_like(state_ref)
    zsum_ref[...] = jnp.zeros_like(zsum_ref)
    maskf = head_mask(F32)
    mask = maskf.astype(BF16)
    ones = jnp.ones((16, width), BF16)
    lower = iota((BLK, width), 1) % BLK <= iota((BLK, width), 0)
    upper = iota((BLK, width), 1) % BLK >= iota((BLK, width), 0)
    nblk = seq // BLK

    def chunk(step, _):
        c = nblk - 1 - step
        at = pl.multiple_of(c * BLK, BLK)
        for g in range(2):
            q = qkv_ref[0, g, pl.ds(at, BLK), :]
            k = qkv_ref[1, g, pl.ds(at, BLK), :]
            v = qkv_ref[2, g, pl.ds(at, BLK), :]
            dn = dn_ref[g, pl.ds(at, BLK), :]
            w = w_ref[g, pl.ds(at, BLK), :]
            state = state_ref[g]
            low = state.astype(BF16)
            zd = zsum_ref[g]
            kb, vb, qb, nb = spread(k, mask), spread(v, mask), spread(q, mask), spread(dn, mask)
            dden = dot(w, mask)
            line = dot_t(ones, spread(w, mask))[0:1]
            da = jnp.where(lower, dot_t(dn, vb) + dden, 0.0).astype(BF16)
            turned = jnp.where(upper, dot_t(k, qb), 0.0).astype(BF16)
            dat = jnp.where(upper, dot_t(v, nb) + line, 0.0).astype(BF16)
            dq = dot_t(dn, s_ref[g, c]) + dden * z_ref[g, c][0:1] + dot(da, kb)
            dk = dot_t(v, low) + zd[0:1] + dot(dat, qb)
            dv = dot(k, low) + dot(turned, nb)
            dr_ref[0, g, pl.ds(at, BLK), :] = (dq * jnp.minimum(q.astype(F32), 1.0)).astype(BF16)
            dr_ref[1, g, pl.ds(at, BLK), :] = (dk * jnp.minimum(k.astype(F32), 1.0)).astype(BF16)
            dr_ref[2, g, pl.ds(at, BLK), :] = dv.astype(BF16)
            state_ref[g] = state + dot(q.T, dn) * maskf
            zsum_ref[g] = zd + jnp.sum(dden * q.astype(F32), axis=0, keepdims=True)
        return 0

    lax.fori_loop(0, nblk, chunk, 0, unroll=2)

    for g in range(2):
        for j in range(4):
            if j < 3:
                both = dot(h1t_ref[...], dr_ref[j, g]).astype(BF16)
            else:
                both = dot(dmt_ref[...], o_ref[g]).astype(BF16)
            for p in range(2):
                where = (p ^ core) if g == 0 else p
                grad_ref[where, g, :, j * part : (j + 1) * part] = both[:, p * part : (p + 1) * part]

    gain = gain_ref[...]

    def finish(t, _):
        at = pl.multiple_of(t * TILE, TILE)
        dh1 = jnp.zeros((TILE, d), F32)
        for g in range(2):
            for j in range(3):
                w = wown_ref[j] if g == 0 else wg_ref[j]
                dh1 = dh1 + dot_t(dr_ref[j, g, pl.ds(at, TILE), :], w)
        xhat, inv = norm_parts(x_ref[pl.ds(at, TILE), :].astype(F32))
        vec_ref[0:1, :] += jnp.sum(dh1 * xhat, axis=0, keepdims=True)
        vec_ref[1:2, :] += jnp.sum(dh1, axis=0, keepdims=True)
        dx = (dm_ref[pl.ds(at, TILE), :] + norm_back(dh1, xhat, inv, gain)).astype(BF16)
        left, right = dx[:, :half], dx[:, half:]
        first = core == 0
        keep_ref[pl.ds(at, TILE), :] = jnp.where(first, left, right)
        send_ref[pl.ds(at, TILE), :] = jnp.where(first, right, left)
        return 0

    lax.fori_loop(0, seq // TILE, finish, 0)


def return_body(ids_ref, spos_ref, mine_ref, other_ref, out_ref):
    core = ids_ref[0]
    seq = mine_ref.shape[0]

    def step(t, _):
        at = pl.multiple_of(t * TILE, TILE)
        where = spos_ref[pl.ds(at, TILE), :]
        lane = iota((TILE, seq), 1)
        a = dot(one_hot(lane + core * seq == where), mine_ref[...])
        b = dot(one_hot(lane + (1 - core) * seq == where), other_ref[...])
        out_ref[pl.ds(at, TILE), :] = (a + b).astype(BF16)
        return 0

    lax.fori_loop(0, 2 * seq // TILE, step, 0)


def arrive_body(place_ref, mine_ref, other_ref, out_ref):
    rows = out_ref.shape[0]
    seq = rows // 2
    half = mine_ref.shape[3]

    def step(t, _):
        at = pl.multiple_of(t * TILE, TILE)
        where = place_ref[pl.ds(at, TILE), :]
        lane = iota((TILE, seq), 1)
        first = one_hot(lane == where)
        second = one_hot(lane + seq == where)
        for side in range(2):
            a = dot(first, mine_ref[:, side].reshape(seq, half))
            b = dot(second, other_ref[:, side].reshape(seq, half))
            out_ref[pl.ds(at, TILE), side * half : (side + 1) * half] = (a + b).astype(BF16)
        return 0

    lax.fori_loop(0, rows // TILE, step, 0)


def per_device(
    tokens,
    seq_lengths,
    packed_slot,
    out_grad,
    qkv_weight,
    out_weight,
    up_weight,
    down_weight,
    gain_first,
    shift_first,
    gain_second,
    shift_second,
    up_bias,
):
    rows, d = tokens.shape
    count = lax.axis_size("dp")
    slot = rows // count
    half = d // 2
    seq = rows // 2
    nblk = seq // BLK
    width = 4 * HD
    part = width // 2
    unit = up_weight.shape[1] // 2
    device = lax.axis_index("dp")
    core = device % 2
    plane = lax.axis_index("tensor")
    ids = jnp.stack([core, plane]).astype(jnp.int32)
    cores = [(i, i ^ 1) for i in range(count)]
    planes = [(0, 1), (1, 0)]

    def swap_core(x):
        return lax.ppermute(x, "dp", cores)

    def swap_plane(x):
        return lax.ppermute(x, "tensor", planes)

    def trade(x):
        return lax.all_to_all(x, "dp", split_axis=0, concat_axis=0, tiled=True)

    def turn(x):
        return x.reshape(1, -1)

    slots_row = packed_slot.reshape(1, rows)
    tok_send, place = call(
        send_tokens_body,
        (shaped((count, slot + HEADER, half), BF16), shaped((1, rows), jnp.int32)),
        in_specs=[SMEM, VMEM, VMEM],
        flops=rows * rows * d,
        moved=rows * d * 3,
    )(ids, slots_row, tokens)
    tok_mine = trade(tok_send)
    grad_send = call(
        send_grads_body,
        shaped((count, slot, half), BF16),
        in_specs=[VMEM, VMEM],
        flops=rows * rows * d,
        moved=rows * d * 3,
    )(place, out_grad)

    qkv_piece = lax.dynamic_slice_in_dim(qkv_weight, core * part, part, axis=2)
    bias_own = up_bias.reshape(2, unit)
    bias_c = lax.dynamic_slice_in_dim(bias_own, core, 1, axis=0)
    bias_hi = bias_c.astype(BF16)
    left = bias_c - bias_hi.astype(F32)
    bias_mid = left.astype(BF16)
    bias_lo = (left - bias_mid.astype(F32)).astype(BF16)
    ffn_piece = jnp.concatenate(
        [
            lax.dynamic_slice_in_dim(up_weight, core * unit, unit, axis=1),
            lax.dynamic_slice_in_dim(down_weight, core * unit, unit, axis=0),
            lax.dynamic_slice_in_dim(out_weight, core * part, part, axis=0),
            bias_hi,
            bias_mid,
            bias_lo,
            jnp.zeros((13, d), BF16),
        ],
        axis=0,
    )
    qkv_a = swap_plane(qkv_piece)
    qkv_b = swap_core(qkv_a)
    ffn_a = swap_plane(ffn_piece)
    ffn_b = swap_core(ffn_a)

    def unpack(p):
        up = p[:d]
        down = p[d : d + unit]
        out = p[d + unit : d + unit + part]
        at = d + unit + part
        bias = p[at : at + 3].astype(F32)
        return up, down, out, bias[0:1] + bias[1:2] + bias[2:3]

    up_a, down_a, out_a, bias_a = unpack(ffn_a)
    up_b, down_b, out_b, bias_b = unpack(ffn_b)
    bias = jnp.concatenate([bias_own, bias_a, bias_b, jnp.zeros((4, unit), F32)], axis=0)

    tok_other = swap_core(tok_mine)
    off = ((device // 2) % (TILE // slot)) * slot
    marks = lax.dynamic_slice_in_dim(tok_mine[:, slot : slot + 2, :], off, slot, axis=2).astype(F32)
    spos = (marks[:, 0] * 128.0 + marks[:, 1]).astype(jnp.int32)
    spos_row = spos.reshape(1, rows)
    spos_col = spos.reshape(rows, 1)

    x, h1, qkv, o, rden, states, zsums, middle = call(
        attend_body,
        (
            shaped((seq, d), BF16),
            shaped((seq, d), BF16),
            shaped((3, 2, seq, width), BF16),
            shaped((2, seq, width), BF16),
            shaped((2, seq, width), F32),
            shaped((2, nblk, width, width), BF16),
            shaped((2, nblk, 8, width), F32),
            shaped((seq, d), F32),
        ),
        scratch=(
            pltpu.VMEM((3, d, width), BF16),
            pltpu.VMEM((width, d), BF16),
            pltpu.VMEM((2, width, width), F32),
            pltpu.VMEM((2, 8, width), F32),
        ),
        in_specs=[SMEM] + [VMEM] * 11,
        flops=8 * 10**9,
        moved=20 * 10**6,
    )(
        ids, spos_row, tok_mine, tok_other, qkv_weight, qkv_a, qkv_b, out_weight, out_a, out_b,
        turn(gain_first), turn(shift_first),
    )

    grad_mine = trade(grad_send)
    grad_other = swap_core(grad_mine)

    out_keep, out_send, dmiddle, ffn_grads, vec2, bvec = call(
        ffn_body,
        (
            shaped((seq, half), BF16),
            shaped((seq, half), BF16),
            shaped((seq, d), F32),
            shaped((2, 2, 2, d, unit), BF16),
            shaped((8, d), F32),
            shaped((8, unit), F32),
        ),
        scratch=(
            pltpu.VMEM((d, seq), BF16),
            pltpu.VMEM((d, seq), BF16),
            pltpu.VMEM((4, seq, unit), BF16),
            pltpu.VMEM((4, seq, unit), BF16),
        ),
        in_specs=[SMEM] + [VMEM] * 13,
        flops=16 * 10**9,
        moved=20 * 10**6,
    )(
        ids, spos_row, grad_mine, grad_other, middle, up_weight, up_a, up_b,
        down_weight, down_a, down_b, bias, turn(gain_second), turn(shift_second),
    )

    place_col = place.reshape(rows, 1)

    def go_back(keep, send):
        other = swap_core(send)
        ordered = call(
            return_body,
            shaped((rows, half), BF16),
            in_specs=[SMEM, VMEM, VMEM, VMEM],
            flops=rows * rows * d,
            moved=rows * d * 3,
        )(ids, spos_col, keep, other)
        mine = trade(ordered.reshape(count, slot, half))
        far = swap_plane(mine)
        return call(
            arrive_body,
            shaped((rows, d), BF16),
            in_specs=[VMEM, VMEM, VMEM],
            flops=2 * rows * rows * d,
            moved=rows * d * 4,
        )(place_col, mine.reshape(count // 2, 2, slot, half), far.reshape(count // 2, 2, slot, half))

    layer_out = go_back(out_keep, out_send)

    groups = [[c + 2 * k for k in range(count // 2)] for c in range(2)]

    def add(a, b):
        return (a.astype(F32) + b.astype(F32)).astype(BF16)

    def reduce(grads, extra):
        kept, sent = grads[0], grads[1]
        shape = kept.shape[1:]
        kept = kept.reshape(2, -1, d)
        sent = sent.reshape(2, -1, d)
        n = kept.shape[1]
        if extra is not None:
            sent = jnp.concatenate([sent.reshape(2 * n, d), extra], axis=0)
            kept = jnp.concatenate([kept.reshape(2 * n, d), extra], axis=0)
        else:
            sent = sent.reshape(2 * n, d)
            kept = kept.reshape(2 * n, d)
        total = add(kept, swap_core(sent))
        own, far = total[:n], total[n:]
        if extra is not None:
            own = jnp.concatenate([own, total[2 * n :]], axis=0)
        own = add(own, swap_plane(far))
        own = lax.psum(own, "dp", axis_index_groups=groups)
        return own[:n].reshape(shape), (own[n:] if extra is not None else None)

    ffn_sum, _ = reduce(ffn_grads, None)

    in_keep, in_send, attn_grads, vec1 = call(
        attend_back_body,
        (
            shaped((seq, half), BF16),
            shaped((seq, half), BF16),
            shaped((2, 2, d, 4 * part), BF16),
            shaped((8, d), F32),
        ),
        scratch=(
            pltpu.VMEM((3, d, width), BF16),
            pltpu.VMEM((width, d), BF16),
            pltpu.VMEM((d, seq), BF16),
            pltpu.VMEM((d, seq), BF16),
            pltpu.VMEM((2, seq, width), BF16),
            pltpu.VMEM((2, seq, width), BF16),
            pltpu.VMEM((3, 2, seq, width), BF16),
            pltpu.VMEM((2, width, width), F32),
            pltpu.VMEM((2, 8, width), F32),
        ),
        in_specs=[SMEM] + [VMEM] * 15,
        flops=12 * 10**9,
        moved=20 * 10**6,
    )(
        ids, dmiddle, out_weight, out_a, out_b, qkv, o, rden, states, zsums,
        h1, x, qkv_weight, qkv_a, qkv_b, turn(gain_first),
    )
    grad_input = go_back(in_keep, in_send)

    pieces = bvec[:4]
    ours = pieces[:2]
    theirs = jnp.where(core == 0, pieces[2:4], pieces[3:1:-1])
    halves = jnp.where(
        plane == 0,
        jnp.concatenate([ours, theirs], axis=0),
        jnp.concatenate([theirs, ours], axis=0),
    )
    extra = jnp.concatenate(
        [vec1[:2], vec2[:2], halves, jnp.zeros((8, d), F32)], axis=0
    ).astype(BF16)
    attn_sum, vec_sum = reduce(attn_grads, extra)

    def both(mine):
        other = swap_core(mine)
        return jnp.where(core == 0, mine, other), jnp.where(core == 0, other, mine)

    ffn0, ffn1 = both(ffn_sum)
    attn0, attn1 = both(attn_sum)
    grad_up = jnp.concatenate([ffn0[0], ffn1[0]], axis=1).astype(F32)
    grad_down = jnp.concatenate([ffn0[1].T, ffn1[1].T], axis=0).astype(F32)
    grad_qkv = jnp.stack(
        [
            jnp.concatenate([attn0[:, j * part : (j + 1) * part], attn1[:, j * part : (j + 1) * part]], axis=1)
            for j in range(3)
        ]
    ).astype(F32)
    grad_outproj = jnp.concatenate([attn0[:, 3 * part :].T, attn1[:, 3 * part :].T], axis=0).astype(F32)
    vec_sum = vec_sum.astype(F32)
    bias_sum = vec_sum[4:8].reshape(2, 2 * unit)
    grad_up_bias = jnp.where(plane == 0, bias_sum[0], bias_sum[1])
    return (
        layer_out,
        grad_input,
        grad_qkv,
        grad_outproj,
        grad_up,
        grad_down,
        vec_sum[0],
        vec_sum[1],
        vec_sum[2],
        vec_sum[3],
        grad_up_bias,
    )


def solution(mesh):
    placed = (
        P("dp", None),
        P("dp"),
        P("dp"),
        P("dp", None),
        P(None, None, "tensor"),
        P("tensor", None),
        P(None, "tensor"),
        P("tensor", None),
        P(),
        P(),
        P(),
        P(),
        P("tensor"),
    )
    return jax.shard_map(
        per_device,
        mesh=mesh,
        in_specs=placed,
        out_specs=(
            P("dp", None),
            P("dp", None),
            P(None, None, "tensor"),
            P("tensor", None),
            P(None, "tensor"),
            P("tensor", None),
            P(),
            P(),
            P(),
            P(),
            P("tensor"),
        ),
        check_vma=False,
    )
```

time: 941 us -> 383 us (0.41)
  waiting for transfers between devices: 427 us -> 161 us
  local copies, waits for them, and re-layouts: 190 us -> 36.4 us
  matrix products: 148 us -> 0 us
  Pallas kernels: 0 us -> 120 us
  blocking collectives: 60.4 us -> 0 us
  other arithmetic: 54 us -> 13.9 us
    psum x4 -> x1, waiting for transfers between devices: 382 us -> 36.2 us  [reduce(): own = lax.psum(own, 'dp', axis_index_groups=groups)]
    dot_general x30 -> x0, matrix products: 148 us -> none  [the longest x3 27.8 us: linear_attention(): jnp.einsum('chij,cjhf->cihf', scores, values, precision=best)]
    pallas_call x0 -> x9, Pallas kernels: none -> 120 us  [the longest x1 27.4 us: per_device(): call(attend_back_body, (shaped((seq, half), BF16), shaped((seq, half), BF...]
    gather x9 -> x0, local copies, waits for them, and re-layouts: 106 us -> none  [the longest x1 20.6 us: per_device(): packed_slot[order].reshape(count, slot)]
    ppermute x0 -> x16, waiting for transfers between devices: none -> 99.1 us  [the longest x6 98.9 us: swap_plane(): return lax.ppermute(x, 'tensor', planes)]
    psum x1 -> x0, blocking collectives: 60.4 us -> none  [per_device(): lax.psum((grad_qkv, grad_outproj, grad_up, grad_down, grad_up_bias, grad_...]
    reshape x8 -> x2, local copies, waits for them, and re-layouts: 35.3 us -> 1.35 us  [the longest x1 1.35 us: per_device(): place_col = place.reshape(rows, 1)]
    reduce_sum x10 -> x0, other arithmetic: 24.4 us -> none  [the longest x3 11.1 us: layer_norm(): return cent * lax.rsqrt(var + 1e-05) * gain + shift]
  transfers between devices with their start and end apart: 9 -> 21, of which waited for: 6 -> 8; matrix products, arithmetic and copies ran while one was open for 17% -> 11% of each run, Pallas kernels for 0% -> 14%
where the time goes in v1:
time: 383 us; the launch traced here: 382 us
  waiting for transfers between devices  161 us (42%)
  Pallas kernels  120 us (31%)
  local copies, waits for them, and re-layouts  36.4 us (10%)
  starting transfers between devices  36.2 us (9%)
  between operations  14.4 us (4%)
  other arithmetic  13.9 us (4%)
    ppermute x6, waiting for transfers between devices, swap_plane(): return lax.ppermute(x, 'tensor', planes)  98.9 us
    psum x1, waiting for transfers between devices, reduce(): own = lax.psum(own, 'dp', axis_index_groups=groups)  36.2 us
    pallas_call x1, Pallas kernels, per_device(): call(attend_back_body, (shaped((seq, half), BF16), shaped((seq, half), BF...  27.4 us
    all_to_all x4, starting transfers between devices, trade(): return lax.all_to_all(x, 'dp', split_axis=0, concat_axis=0, tiled=True)  27.1 us
    pallas_call x1, Pallas kernels, per_device(): call(ffn_body, (shaped((seq, half), BF16), shaped((seq, half), BF16), sha...  25.4 us
    all_to_all x4, waiting for transfers between devices, trade(): return lax.all_to_all(x, 'dp', split_axis=0, concat_axis=0, tiled=True)  25.4 us
    pallas_call x1, Pallas kernels, per_device(): call(attend_body, (shaped((seq, d), BF16), shaped((seq, d), BF16), shaped...  24.2 us
    pallas_call x2, Pallas kernels, go_back(): call(arrive_body, shaped((rows, d), BF16), in_specs=[VMEM, VMEM, VMEM], f...  18.3 us
  transfers between devices with their start and end apart: 21, of which 8 were waited for; matrix products, arithmetic and copies ran while one was open for 11% of the time, Pallas kernels for 14%

profile of v1, /device:TPU:0, one launch (start us, length us, event | category | flops | bytes accessed | tf_op | source)
XLA Modules:
  0.0 381.5 jit_solution(6545675877240006939)
XLA Ops:
  7.2 0.6 pad_add_fusion.ids_ref
  7.8 6.6 %shard_map.203 = (bf16[16,136,256]{2,1,0:T(8,128)(2,1)}, s32[1,2048]{1,0:T(1,128)}) custom-call(s32[2]{0:T(128)} %pad_add_fusion.ids_ref, s32[1,2048]{1,0:T(1,128)} %bitcast.67, bf16[2048,512]{1,0:T(8,128)(2,1)} %tok_ref.2), custom_call_target="tpu_custom_call" | custom-call | flops 2147483648 | bytes 3145728 | tf_op jit(solution)/shard_map/pallas_call | solution.py:486
  14.4 5.4 %shard_map.204 = bf16[16,128,256]{2,1,0:T(8,128)(2,1)} custom-call(s32[1,2048]{1,0:T(1,128)} %get-tuple-element.31.place_ref, bf16[2048,512]{1,0:T(8,128)(2,1)} %tok_ref.3), custom_call_target="tpu_custom_call" | custom-call | flops 2147483648 | bytes 3145728 | tf_op jit(solution)/shard_map/pallas_call | solution.py:494
  19.8 7.5 %all-to-all-start.1 = ((bf16[16,128,256]{2,1,0:T(8,128)(2,1)}), bf16[16,128,256]{2,1,0:T(8,128)(2,1)S(1)}, u32[]{:S(2)}, u32[]{:S(2)}) async-start(bf16[16,128,256]{2,1,0:T(8,128)(2,1)} %shard_map.204), calls=%async_computation.1 | async-start | bytes 2097152 | tf_op jit(solution)/shard_map/all_to_all | solution.py:480
  27.4 22.8 %all-to-all-done.1.mine_ref = bf16[16,128,256]{2,1,0:T(8,128)(2,1)S(1)} async-done(((bf16[16,128,256]{2,1,0:T(8,128)(2,1)}), bf16[16,128,256]{2,1,0:T(8,128)(2,1)S(1)}, u32[]{:S(2)}, u32[]{:S(2)}) %all-to-all-start.1) | async-done | bytes 1048608 | tf_op jit(solution)/shard_map/all_to_all | solution.py:480
  50.2 6.9 %all-to-all-start = ((bf16[16,136,256]{2,1,0:T(8,128)(2,1)}), bf16[16,136,256]{2,1,0:T(8,128)(2,1)}, u32[]{:S(2)}, u32[]{:S(2)}) async-start(bf16[16,136,256]{2,1,0:T(8,128)(2,1)} %get-tuple-element.32), calls=%async_computation | async-start | bytes 2228224 | tf_op jit(solution)/shard_map/all_to_all | solution.py:480
  57.2 1.1 constant_dynamic-slice_fusion.2
  58.8 1.6 collective-permute-start.4
  60.4 1.8 constant_dynamic-slice_fusion.4
  62.7 33.2 %collective-permute-done.2.wa_ref = bf16[3,512,128]{2,1,0:T(8,128)(2,1)} collective-permute-done((bf16[3,512,128]{2,1,0:T(8,128)(2,1)}, bf16[3,512,128]{2,1,0:T(8,128)(2,1)}, u32[]{:S(2)}, u32[]{:S(2)}) %collective-permute-start.2) | collective-permute-done | bytes 393248 | tf_op jit(solution)/shard_map/ppermute | solution.py:477
  96.0 0.5 collective-permute-start.5
  96.5 0.7 slice.214.oa_ref
  97.2 1.0 fusion.9
  98.2 0.9 slice.211
  99.1 0.6 collective-permute-start.1
  99.6 0.6 fusion.12.spos_ref
  100.3 0.7 maximum_maximum_fusion.bias_ref
  100.9 0.6 slice.215.ob_ref
  101.6 1.0 fusion.8
  102.7 1.0 copy-done.6
  103.7 24.2 %shard_map.205 = (bf16[1024,512]{1,0:T(8,128)(2,1)}, bf16[1024,512]{1,0:T(8,128)(2,1)}, bf16[3,2,1024,256]{3,2,1,0:T(8,128)(2,1)}, bf16[2,1024,256]{2,1,0:T(8,12...) custom-call(s32[2]{0:T(128)} %pad_add_fusion.ids_ref, ...), custom_call_target="tpu_custom_call" | custom-call | flops 8000000000 | bytes 20000000 | tf_op jit(solution)/shard_map/pallas_call | solution.py:545
  127.9 25.4 %shard_map.206 = (bf16[1024,256]{1,0:T(8,128)(2,1)}, bf16[1024,256]{1,0:T(8,128)(2,1)}, f32[1024,512]{1,0:T(8,128)}, bf16[2,2,2,512,512]{4,3,2,1,0:T(8,128)(2,1)}, f32[8,512]{1,0:T(8,128)}, /*index=5*/f32[8,512]{1,0:T(8,128)}) custom-call(s32[2]{0:T(128)} %pad_add_fusion.ids_ref, s32[1,2048]{1,0:T(1,128)} %fusion.12.spos_ref, ...), custom_call_target="tpu_custom_call" | custom-call | flops 16000000000 | bytes 20000000 | tf_op jit(solution)/shard_map/pallas_call | solution.py:574
  153.3 27.4 %shard_map.209 = (bf16[1024,256]{1,0:T(8,128)(2,1)}, bf16[1024,256]{1,0:T(8,128)(2,1)}, bf16[2,2,512,512]{3,2,1,0:T(8,128)(2,1)}, f32[8,512]{1,0:T(8,128)}) custom-call(s32[2]{0:T(128)} %pad_add_fusion.ids_ref, f32[1024,512]{1,0:T(8,128)} %get-tuple-element.36.dm_ref, bf16[256,512]{1,0:T(8,128)(2,1)} %oown_ref.3, bf16[128,512]{1,0:T(8,128)(2,1)} %slice.214.oa_ref, ...), custom_call_target="tpu_custom_call" | custom-call | flops 12000000000 | bytes 20000000 | tf_op jit(solution)/shard_map/pallas_call | solution.py:648
  180.9 1.3 copy.48.spos_ref
  182.2 3.9 %fusion.6 = (bf16[1,2,2,512,512]{4,3,2,1,0:T(8,128)(2,1)S(1)}, bf16[1,2,2,512,512]{4,3,2,1,0:T(8,128)(2,1)}) fusion(bf16[2,2,2,512,512]{4,3,2,1,0:T(8,128)(2,1)} %get-tuple-element.50), kind=kLoop, calls=%fused_computation.51 | loop fusion | bytes 8388608 | tf_op jit(solution)/shard_map/slice | solution.py:627
  186.5 0.8 copy-done.9
  187.3 6.3 %shard_map.210 = bf16[2048,256]{1,0:T(8,128)(2,1)} custom-call(s32[2]{0:T(128)} %pad_add_fusion.ids_ref, s32[2048,1]{1,0:T(8,128)} %copy.48.spos_ref, bf16[1024,256]{1,0:T(8,128)(2,1)} %get-tuple-element.44.mine_ref, bf16[1024,256]{1,0:T(8,128)(2,1)} %copy-done.9), custom_call_target="tpu_custom_call" | custom-call | flops 2147483648 | bytes 3145728 | tf_op jit(solution)/shard_map/pallas_call | solution.py:602
  193.7 5.8 %all-to-all-start.3 = ((bf16[16,128,256]{2,1,0:T(8,128)(2,1)}), bf16[16,128,256]{2,1,0:T(8,128)(2,1)}, u32[]{:S(2)}, u32[]{:S(2)}) async-start(bf16[16,128,256]{2,1,0:T(8,128)(2,1)} %bitcast.58), calls=%async_computation.3 | async-start | bytes 2097152 | tf_op jit(solution)/shard_map/all_to_all | solution.py:480
  199.5 0.7 slice.182
  200.3 0.7 slice.291
  201.0 0.7 slice.290
  202.1 0.8 fusion.11
  202.9 2.7 fusion.7
  205.7 4.0 %concatenate.48 = bf16[1040,512]{1,0:T(8,128)(2,1)} concatenate(bf16[1024,512]{1,0:T(8,128)(2,1)S(1)} %bitcast.56, bf16[2,512]{1,0:T(2,128)(2,1)S(1)} %slice.291, bf16[2,512]{1,0:T(2,128)(2,1)S(1)} %slice.290, bf16[4,512]{1,0:T(4,128)(2,1)S(1)} %fusion.2, bf16[8,512]{1,0:T(8,128)(2,1)S(1)} %broadcast_in_dim.11), dimensions={0} | concatenate | bytes 2129920 | tf_op jit(solution)/shard_map/concatenate | solution.py:633
  209.8 3.8 concatenate.47
  213.6 6.3 %shard_map.207 = bf16[2048,256]{1,0:T(8,128)(2,1)} custom-call(s32[2]{0:T(128)} %pad_add_fusion.ids_ref, s32[2048,1]{1,0:T(8,128)} %copy.48.spos_ref, bf16[1024,256]{1,0:T(8,128)(2,1)} %get-tuple-element.34.mine_ref, bf16[1024,256]{1,0:T(8,128)(2,1)} %collective-permute-done.6.other_ref), custom_call_target="tpu_custom_call" | custom-call | flops 2147483648 | bytes 3145728 | tf_op jit(solution)/shard_map/pallas_call | solution.py:602
  220.0 2.5 all-to-all-done.3
  222.5 6.9 %all-to-all-start.2 = ((bf16[16,128,256]{2,1,0:T(8,128)(2,1)}), bf16[16,128,256]{2,1,0:T(8,128)(2,1)}, u32[]{:S(2)}, u32[]{:S(2)}) async-start(bf16[16,128,256]{2,1,0:T(8,128)(2,1)} %bitcast.57), calls=%async_computation.2 | async-start | bytes 2097152 | tf_op jit(solution)/shard_map/all_to_all | solution.py:480
  229.5 2.2 fusion
  231.7 1.6 collective-permute-start.14
  233.3 1.5 add_convert_fusion
  234.9 0.6 collective-permute-start.11
  235.5 33.3 %collective-permute-done.11 = bf16[528,512]{1,0:T(8,128)(2,1)S(1)} collective-permute-done((bf16[528,512]{1,0:T(8,128)(2,1)S(1)}, bf16[528,512]{1,0:T(8,128)(2,1)S(1)}, u32[]{:S(2)}, u32[]{:S(2)}) %collective-permute-start.11) | collective-permute-done | bytes 540704 | tf_op jit(solution)/shard_map/ppermute | solution.py:477
  268.8 1.0 add_convert_fusion.2
  269.8 1.5 collective-permute-start.9
  271.3 1.3 add_convert_fusion.1
  272.6 0.6 collective-permute-start.7
  273.2 1.3 copy.49.place_ref
  274.5 21.5 %collective-permute-done.9 = bf16[16,128,256]{2,1,0:T(8,128)(2,1)S(1)} collective-permute-done((bf16[16,128,256]{2,1,0:T(8,128)(2,1)}, bf16[16,128,256]{2,1,0:T(8,128)(2,1)S(1)}, u32[]{:S(2)}, u32[]{:S(2)}) %collective-permute-start.9) | collective-permute-done | bytes 1048608 | tf_op jit(solution)/shard_map/ppermute | solution.py:477
  296.1 1.0 copy-done.7
  297.0 9.2 %shard_map.211 = bf16[2048,512]{1,0:T(8,128)(2,1)} custom-call(s32[2048,1]{1,0:T(8,128)} %copy.49.place_ref, bf16[8,2,128,256]{3,2,1,0:T(8,128)(2,1)} %bitcast.14.mine_ref, bf16[8,2,128,256]{3,2,1,0:T(8,128)(2,1)} %bitcast.65), custom_call_target="tpu_custom_call" | custom-call | flops 4294967296 | bytes 4194304 | tf_op jit(solution)/shard_map/pallas_call | solution.py:611
  306.2 10.9 %collective-permute-done.7 = bf16[16,128,256]{2,1,0:T(8,128)(2,1)S(1)} collective-permute-done((bf16[16,128,256]{2,1,0:T(8,128)(2,1)}, bf16[16,128,256]{2,1,0:T(8,128)(2,1)S(1)}, u32[]{:S(2)}, u32[]{:S(2)}) %collective-permute-start.7) | collective-permute-done | bytes 1048608 | tf_op jit(solution)/shard_map/ppermute | solution.py:477
  317.1 1.0 copy-done.8
  318.0 9.2 %shard_map.208 = bf16[2048,512]{1,0:T(8,128)(2,1)} custom-call(s32[2048,1]{1,0:T(8,128)} %copy.49.place_ref, bf16[8,2,128,256]{3,2,1,0:T(8,128)(2,1)} %bitcast.11.mine_ref, bf16[8,2,128,256]{3,2,1,0:T(8,128)(2,1)} %bitcast.66), custom_call_target="tpu_custom_call" | custom-call | flops 4294967296 | bytes 4194304 | tf_op jit(solution)/shard_map/pallas_call | solution.py:611
  327.2 36.2 %all-reduce.3.cloned.1.call-done = (bf16[528,512]{1,0:T(8,128)(2,1)}, bf16[2,512,512]{2,1,0:T(8,128)(2,1)}) async-done(((bf16[528,512]{1,0:T(8,128)(2,1)}, bf16[2,512,512]{2,1,0:T(8,128)(2,1)}), (bf16[528,512]{1,0:T(8,128)(2,1)}, bf16[2,512,512]{2,1,0:T(8,128)(2,1)})) %all-reduce.3.cloned.1.call-update) | async-done | bytes 1589264 | tf_op jit(solution)/shard_map/psum | solution.py:643
  363.4 1.1 slice.233
  364.6 0.7 slice_convert_fusion
  365.8 0.6 copy.54
  366.4 0.6 fusion.10
  367.0 1.1 broadcast_select_fusion.3
  368.4 1.0 copy.52
  369.5 1.3 maximum_convert_fusion.2
  371.3 1.8 copy.53
  373.1 1.6 maximum_convert_fusion
  (73 shorter events, 4.1 us)
Async XLA Ops:
  19.8 7.5 %copy-start.5 = (f32[1024]{0:T(1024)S(1)}, f32[1024]{0:T(1024)}, u32[]{:S(2)}) copy-start(f32[1024]{0:T(1024)} %param.24) | copy-start | bytes 12292
  19.8 7.6 %copy-start.3 = (bf16[256,512]{1,0:T(8,128)(2,1)S(1)}, bf16[256,512]{1,0:T(8,128)(2,1)}, u32[]{:S(2)}) copy-start(bf16[256,512]{1,0:T(8,128)(2,1)} %oown_ref.3) | copy-start | bytes 786436
  19.8 37.4 %copy-start.2 = (bf16[1024,512]{1,0:T(8,128)(2,1)S(1)}, bf16[1024,512]{1,0:T(8,128)(2,1)}, u32[]{:S(2)}) copy-start(bf16[1024,512]{1,0:T(8,128)(2,1)} %down_ref.1) | copy-start | bytes 3145732
  19.8 30.4 %all-to-all-start.1 = ((bf16[16,128,256]{2,1,0:T(8,128)(2,1)}), bf16[16,128,256]{2,1,0:T(8,128)(2,1)S(1)}, u32[]{:S(2)}, u32[]{:S(2)}) async-start(bf16[16,128,256]{2,1,0:T(8,128)(2,1)} %shard_map.204), calls=%async_computation.1 | async-start | bytes 2097152 | tf_op jit(solution)/shard_map/all_to_all | solution.py:480
  50.2 48.0 %copy-start.1 = (bf16[16,128,256]{2,1,0:T(8,128)(2,1)}, bf16[16,128,256]{2,1,0:T(8,128)(2,1)S(1)}, u32[]{:S(2)}) copy-start(bf16[16,128,256]{2,1,0:T(8,128)(2,1)S(1)} %all-to-all-done.1.mine_ref) | copy-start | bytes 3145732
  50.2 48.0 %all-to-all-start = ((bf16[16,136,256]{2,1,0:T(8,128)(2,1)}), bf16[16,136,256]{2,1,0:T(8,128)(2,1)}, u32[]{:S(2)}, u32[]{:S(2)}) async-start(bf16[16,136,256]{2,1,0:T(8,128)(2,1)} %get-tuple-element.32), calls=%async_computation | async-start | bytes 2228224 | tf_op jit(solution)/shard_map/all_to_all | solution.py:480
  58.8 37.2 %collective-permute-start.4 = (bf16[1168,512]{1,0:T(8,128)(2,1)S(1)}, bf16[1168,512]{1,0:T(8,128)(2,1)S(1)}, u32[]{:S(2)}, u32[]{:S(2)}) collective-permute-start(bf16[1168,512]{1,0:T(8,128)(2,1)S(1)} %concatenate.43), channel_id=1, source_target_pairs={{0,1},{1,0},{2,3},{3,2},{4,5},{5,4},{6,7},{7,6},{8,9},{9,8},{10,11... | collective-permute-start | bytes 3588104 | tf_op jit(solution)/shard_map/ppermute | solution.py:477
  62.2 33.8 %collective-permute-start.2 = (bf16[3,512,128]{2,1,0:T(8,128)(2,1)}, bf16[3,512,128]{2,1,0:T(8,128)(2,1)}, u32[]{:S(2)}, u32[]{:S(2)}) collective-permute-start(bf16[3,512,128]{2,1,0:T(8,128)(2,1)} %constant_dynamic-slice_fusion.4), channel_id=1, source_target_pairs={{0,1},{1,0},{2,3},{3,2},{4,5},{5,4},{6,7},{7,6},{8,9},{9,8},{10,11... | collective-permute-start | bytes 1179656 | tf_op jit(solution)/shard_map/ppermute | solution.py:477
  96.0 6.6 %collective-permute-start.3 = (bf16[3,512,128]{2,1,0:T(8,128)(2,1)}, bf16[3,512,128]{2,1,0:T(8,128)(2,1)}, u32[]{:S(2)}, u32[]{:S(2)}) collective-permute-start(bf16[3,512,128]{2,1,0:T(8,128)(2,1)} %collective-permute-done.2.wa_ref), channel_id=1, source_target_pairs={{0,2},{2,0},{4,6},{6,4},{8,10},{10,8},{12,14},{14,12},{16,18},{18,... | collective-permute-start | bytes 1179656 | tf_op jit(solution)/shard_map/ppermute | solution.py:474
  96.0 4.3 %collective-permute-start.5 = (bf16[1168,512]{1,0:T(8,128)(2,1)S(1)}, bf16[1168,512]{1,0:T(8,128)(2,1)S(1)}, u32[]{:S(2)}, u32[]{:S(2)}) collective-permute-start(bf16[1168,512]{1,0:T(8,128)(2,1)S(1)} %collective-permute-done.4), channel_id=1, source_target_pairs={{0,2},{2,0},{4,6},{6,4},{8,10},{10,8},{12,14},{14,12},{16,18},{18,... | collective-permute-start | bytes 3588104 | tf_op jit(solution)/shard_map/ppermute | solution.py:474
  98.2 29.7 %collective-permute-start = (bf16[16,128,256]{2,1,0:T(8,128)(2,1)S(1)}, bf16[16,128,256]{2,1,0:T(8,128)(2,1)}, u32[]{:S(2)}, u32[]{:S(2)}) collective-permute-start(bf16[16,128,256]{2,1,0:T(8,128)(2,1)S(1)} %all-to-all-done.1.mine_ref), channel_id=1, source_target_pairs={{0,2},{2,0},{4,6},{6,4},{8,10},{10,8},{12,14},{14,12},{16,18},{18,... | collective-permute-start | bytes 3145736 | tf_op jit(solution)/shard_map/ppermute | solution.py:474
  99.1 3.6 collective-permute-start.1
  102.7 1.0 copy-start.6
  180.7 5.8 %collective-permute-start.8 = (bf16[1024,256]{1,0:T(8,128)(2,1)}, bf16[1024,256]{1,0:T(8,128)(2,1)S(1)}, u32[]{:S(2)}, u32[]{:S(2)}) collective-permute-start(bf16[1024,256]{1,0:T(8,128)(2,1)} %get-tuple-element.45), channel_id=1, source_target_pairs={{0,2},{2,0},{4,6},{6,4},{8,10},{10,8},{12,14},{14,12},{16,18},{18,... | collective-permute-start | bytes 1572872 | tf_op jit(solution)/shard_map/ppermute | solution.py:474
  186.2 43.3 %collective-permute-start.13 = (bf16[2048,512]{1,0:T(8,128)(2,1)}, bf16[2048,512]{1,0:T(8,128)(2,1)}, u32[]{:S(2)}, u32[]{:S(2)}) collective-permute-start(bf16[2048,512]{1,0:T(8,128)(2,1)} %bitcast.24), channel_id=1, source_target_pairs={{0,2},{2,0},{4,6},{6,4},{8,10},{10,8},{12,14},{14,12},{16,18},{18,... | collective-permute-start | bytes 6291464 | tf_op jit(solution)/shard_map/ppermute | solution.py:474
  186.5 0.8 copy-start.9
  193.7 28.8 %all-to-all-start.3 = ((bf16[16,128,256]{2,1,0:T(8,128)(2,1)}), bf16[16,128,256]{2,1,0:T(8,128)(2,1)}, u32[]{:S(2)}, u32[]{:S(2)}) async-start(bf16[16,128,256]{2,1,0:T(8,128)(2,1)} %bitcast.58), calls=%async_computation.3 | async-start | bytes 2097152 | tf_op jit(solution)/shard_map/all_to_all | solution.py:480
  201.8 11.8 %collective-permute-start.6 = (bf16[1024,256]{1,0:T(8,128)(2,1)}, bf16[1024,256]{1,0:T(8,128)(2,1)}, u32[]{:S(2)}, u32[]{:S(2)}) collective-permute-start(bf16[1024,256]{1,0:T(8,128)(2,1)} %get-tuple-element.35), channel_id=1, source_target_pairs={{0,2},{2,0},{4,6},{6,4},{8,10},{10,8},{12,14},{14,12},{16,18},{18,... | collective-permute-start | bytes 1572872 | tf_op jit(solution)/shard_map/ppermute | solution.py:474
  209.6 23.7 %collective-permute-start.10 = (bf16[1040,512]{1,0:T(8,128)(2,1)}, bf16[1040,512]{1,0:T(8,128)(2,1)}, u32[]{:S(2)}, u32[]{:S(2)}) collective-permute-start(bf16[1040,512]{1,0:T(8,128)(2,1)} %concatenate.48), channel_id=1, source_target_pairs={{0,2},{2,0},{4,6},{6,4},{8,10},{10,8},{12,14},{14,12},{16,18},{18,... | collective-permute-start | bytes 3194888 | tf_op jit(solution)/shard_map/ppermute | solution.py:474
  222.5 50.1 %all-to-all-start.2 = ((bf16[16,128,256]{2,1,0:T(8,128)(2,1)}), bf16[16,128,256]{2,1,0:T(8,128)(2,1)}, u32[]{:S(2)}, u32[]{:S(2)}) async-start(bf16[16,128,256]{2,1,0:T(8,128)(2,1)} %bitcast.57), calls=%async_computation.2 | async-start | bytes 2097152 | tf_op jit(solution)/shard_map/all_to_all | solution.py:480
  229.4 134.0 %all-reduce.3.cloned.1.call-start = ((), (), s32[]{:S(2)}) async-start(), calls=%async_computation.4 | async-start | bytes 3178496 | tf_op jit(solution)/shard_map/psum | solution.py:643
  231.7 39.6 %collective-permute-start.14 = (bf16[1024,512]{1,0:T(8,128)(2,1)S(1)}, bf16[1024,512]{1,0:T(8,128)(2,1)S(1)}, u32[]{:S(2)}, u32[]{:S(2)}) collective-permute-start(bf16[1024,512]{1,0:T(8,128)(2,1)S(1)} %slice.243), channel_id=1, source_target_pairs={{0,1},{1,0},{2,3},{3,2},{4,5},{5,4},{6,7},{7,6},{8,9},{9,8},{10,11... | collective-permute-start | bytes 3145736 | tf_op jit(solution)/shard_map/ppermute | solution.py:477
  234.9 33.9 %collective-permute-start.11 = (bf16[528,512]{1,0:T(8,128)(2,1)S(1)}, bf16[528,512]{1,0:T(8,128)(2,1)S(1)}, u32[]{:S(2)}, u32[]{:S(2)}) collective-permute-start(bf16[528,512]{1,0:T(8,128)(2,1)S(1)} %slice.232), channel_id=1, source_target_pairs={{0,1},{1,0},{2,3},{3,2},{4,5},{5,4},{6,7},{7,6},{8,9},{9,8},{10,11... | collective-permute-start | bytes 1622024 | tf_op jit(solution)/shard_map/ppermute | solution.py:477
  269.8 3.4 copy-start.4
  269.8 26.3 %collective-permute-start.9 = (bf16[16,128,256]{2,1,0:T(8,128)(2,1)}, bf16[16,128,256]{2,1,0:T(8,128)(2,1)S(1)}, u32[]{:S(2)}, u32[]{:S(2)}) collective-permute-start(bf16[16,128,256]{2,1,0:T(8,128)(2,1)} %all-to-all-done.3), channel_id=1, source_target_pairs={{0,1},{1,0},{2,3},{3,2},{4,5},{5,4},{6,7},{7,6},{8,9},{9,8},{10,11... | collective-permute-start | bytes 3145736 | tf_op jit(solution)/shard_map/ppermute | solution.py:477
  272.6 44.5 %collective-permute-start.7 = (bf16[16,128,256]{2,1,0:T(8,128)(2,1)}, bf16[16,128,256]{2,1,0:T(8,128)(2,1)S(1)}, u32[]{:S(2)}, u32[]{:S(2)}) collective-permute-start(bf16[16,128,256]{2,1,0:T(8,128)(2,1)} %all-to-all-done.2), channel_id=1, source_target_pairs={{0,1},{1,0},{2,3},{3,2},{4,5},{5,4},{6,7},{7,6},{8,9},{9,8},{10,11... | collective-permute-start | bytes 3145736 | tf_op jit(solution)/shard_map/ppermute | solution.py:477
  296.0 1.0 copy-start.7
  317.0 1.0 copy-start.8
  364.5 2.5 collective-permute-start.12
  365.3 5.4 %collective-permute-start.15 = (bf16[2,512,512]{2,1,0:T(8,128)(2,1)}, bf16[2,512,512]{2,1,0:T(8,128)(2,1)S(1)}, u32[]{:S(2)}, u32[]{:S(2)}) collective-permute-start(bf16[2,512,512]{2,1,0:T(8,128)(2,1)} %get-tuple-element.85), channel_id=1, source_target_pairs={{0,2},{2,0},{4,6},{6,4},{8,10},{10,8},{12,14},{14,12},{16,18},{18,... | collective-permute-start | bytes 3145736 | tf_op jit(solution)/shard_map/ppermute | solution.py:474
  369.4 1.4 copy-start
Sparse Core Ops, SparseCore 0:
  272.7 90.6 all-reduce.2

commit v2 on v1

--- a/solution.py
+++ b/solution.py
@@ -150,8 +150,20 @@
     return jnp.concatenate([x, x, x, x], axis=0) * mask
 
 
+def unpack_heads(wa_ref, wb_ref, wg_ref, og_ref):
+    part = wa_ref.shape[2]
+    for j in range(3):
+        wg_ref[j, :, 0:part] = wa_ref[j]
+        wg_ref[j, :, part : 2 * part] = wb_ref[j]
+    for side, ref in enumerate((wa_ref, wb_ref)):
+        for k in range(og_ref.shape[1] // part):
+            og_ref[side * part : (side + 1) * part, k * part : (k + 1) * part] = ref[
+                3, k * part : (k + 1) * part, :
+            ]
+
+
 def attend_body(
-    ids_ref, spos_ref, mine_ref, other_ref, wown_ref, wa_ref, wb_ref, oown_ref, oa_ref, ob_ref,
+    ids_ref, spos_ref, mine_ref, other_ref, wown_ref, wa_ref, wb_ref, oown_ref,
     gain_ref, shift_ref,
     x_ref, h1_ref, qkv_ref, o_ref, rden_ref, s_ref, z_ref, m_ref,
     wg_ref, og_ref, state_ref, zsum_ref,
@@ -161,11 +173,7 @@
     rows = count * slot
     seq = rows // 2
     width = 4 * HD
-    for j in range(3):
-        wg_ref[j, :, 0 : width // 2] = wa_ref[j]
-        wg_ref[j, :, width // 2 : width] = wb_ref[j]
-    og_ref[0 : width // 2, :] = oa_ref[...]
-    og_ref[width // 2 : width, :] = ob_ref[...]
+    unpack_heads(wa_ref, wb_ref, wg_ref, og_ref)
     spos = spos_ref[...]
     gain, shift = gain_ref[...], shift_ref[...]
 
@@ -232,23 +240,31 @@
 def ffn_body(
     ids_ref, spos_ref, mine_ref, other_ref, m_ref, uown_ref, ua_ref, ub_ref,
     down_ref, da_ref, db_ref, bias_ref, gain_ref, shift_ref,
-    keep_ref, send_ref, dm_ref, grad_ref, vec_ref, bvec_ref,
+    keep_ref, send_ref, dm_ref, gkeep_ref, gsend_ref, vec_ref, bvec_ref,
     gpt_ref, h2t_ref, rl_ref, du_ref,
 ):
     core = ids_ref[0]
     count, slot, half = mine_ref.shape
     rows = count * slot
     seq = rows // 2
-    unit = ua_ref.shape[1]
+    d, unit = m_ref.shape[1], ua_ref.shape[1]
     spos = spos_ref[...]
     gain, shift = gain_ref[...], shift_ref[...]
     vec_ref[...] = jnp.zeros_like(vec_ref)
     bvec_ref[...] = jnp.zeros_like(bvec_ref)
 
+    far = []
+    for ref in (ua_ref, ub_ref):
+        three = ref[d : d + 16, :].astype(F32)
+        far.append(three[0:1] + three[1:2] + three[2:3])
+
+    def bias_piece(j):
+        return bias_ref[j : j + 1, :] if j < 2 else far[j - 2]
+
     def up_piece(j):
         if j < 2:
             return uown_ref[:, j * unit : (j + 1) * unit]
-        return ua_ref[...] if j == 2 else ub_ref[...]
+        return ua_ref[0:d, :] if j == 2 else ub_ref[0:d, :]
 
     def down_piece(j):
         if j < 2:
@@ -269,7 +285,7 @@
         dh2 = jnp.zeros((TILE, m.shape[1]), F32)
         for j in range(4):
             up, down = up_piece(j), down_piece(j)
-            u = dot(h2, up) + bias_ref[j : j + 1, :]
+            u = dot(h2, up) + bias_piece(j)
             sig = jax.nn.sigmoid(u)
             rl = (u * sig).astype(BF16)
             rl_ref[j, pl.ds(at, TILE), :] = rl
@@ -291,29 +307,25 @@
 
     lax.fori_loop(0, seq // TILE, tile, 0)
 
-    for j in range(4):
-        where = (j ^ core) if j < 2 else j - 2
-        side = 0 if j < 2 else 1
-        grad_ref[where, side, 0] = dot(h2t_ref[...], du_ref[j]).astype(BF16)
-        grad_ref[where, side, 1] = dot(gpt_ref[...], rl_ref[j]).astype(BF16)
+    for to_ref, side, j in ((gsend_ref, 1, 3), (gkeep_ref, 1, 2), (gsend_ref, 0, 1 - core), (gkeep_ref, 0, core)):
+        to_ref[0, side] = dot(h2t_ref[...], du_ref[j]).astype(BF16)
+        to_ref[1, side] = dot(gpt_ref[...], rl_ref[j]).astype(BF16)
 
 
 def attend_back_body(
-    ids_ref, dm_ref, oown_ref, oa_ref, ob_ref, qkv_ref, o_ref, rden_ref, s_ref, z_ref,
-    h1_ref, x_ref, wown_ref, wa_ref, wb_ref, gain_ref,
-    keep_ref, send_ref, grad_ref, vec_ref,
-    wg_ref, og_ref, dmt_ref, h1t_ref, dn_ref, w_ref, dr_ref, state_ref, zsum_ref,
+    ids_ref, dm_ref, oown_ref, qkv_ref, o_ref, rden_ref, s_ref, z_ref,
+    h1_ref, x_ref, wown_ref, wa_ref, wb_ref, gain_ref, vec2_ref, bvec_ref,
+    keep_ref, send_ref, gkeep_ref, gsend_ref,
+    wg_ref, og_ref, dmt_ref, h1t_ref, dn_ref, w_ref, dr_ref, state_ref, zsum_ref, vec_ref,
 ):
     core = ids_ref[0]
     seq, d = dm_ref.shape
     width = 4 * HD
     part = width // 2
     half = keep_ref.shape[1]
-    for j in range(3):
-        wg_ref[j, :, 0:part] = wa_ref[j]
-        wg_ref[j, :, part:width] = wb_ref[j]
-    og_ref[0:part, :] = oa_ref[...]
-    og_ref[part:width, :] = ob_ref[...]
+    lines = gkeep_ref.shape[2]
+    cut = min(d, lines)
+    unpack_heads(wa_ref, wb_ref, wg_ref, og_ref)
     vec_ref[...] = jnp.zeros_like(vec_ref)
 
     def start(t, _):
@@ -377,9 +389,15 @@
                 both = dot(h1t_ref[...], dr_ref[j, g]).astype(BF16)
             else:
                 both = dot(dmt_ref[...], o_ref[g]).astype(BF16)
-            for p in range(2):
-                where = (p ^ core) if g == 0 else p
-                grad_ref[where, g, :, j * part : (j + 1) * part] = both[:, p * part : (p + 1) * part]
+            left, right = both[:, :part], both[:, part:]
+            first = core == 0
+            kept = jnp.where(first, left, right) if g == 0 else left
+            sent = jnp.where(first, right, left) if g == 0 else right
+            for to_ref, value in ((gkeep_ref, kept), (gsend_ref, sent)):
+                lanes = slice(j * part, (j + 1) * part)
+                to_ref[0, g, 0:cut, lanes] = value[0:cut]
+                if cut < d:
+                    to_ref[1, g, 0 : d - cut, lanes] = value[cut:d]
 
     gain = gain_ref[...]
 
@@ -402,6 +420,21 @@
 
     lax.fori_loop(0, seq // TILE, finish, 0)
 
+    plane = ids_ref[1]
+    row = iota((16, d), 0)
+    block = jnp.zeros((16, d), F32)
+    for line, value in enumerate((vec_ref[0:1, :], vec_ref[1:2, :], vec2_ref[0:1, :], vec2_ref[1:2, :])):
+        block = jnp.where(row == line, value, block)
+    for j in range(4):
+        at = 4 + 2 * plane + j if j < 2 else 6 - 2 * plane + (core if j == 2 else 1 - core)
+        block = jnp.where(row == at, bvec_ref[j : j + 1, :], block)
+    low = block.astype(BF16)
+    for ref in (gkeep_ref, gsend_ref):
+        for g in range(2):
+            if lines > d - cut + 16:
+                ref[1, g, d - cut + 16 :, :] = jnp.zeros((lines - d + cut - 16, d), BF16)
+            ref[1, g, d - cut : d - cut + 16, :] = low
+
 
 def return_body(ids_ref, spos_ref, mine_ref, other_ref, out_ref):
     core = ids_ref[0]
@@ -419,7 +452,8 @@
     lax.fori_loop(0, 2 * seq // TILE, step, 0)
 
 
-def arrive_body(place_ref, mine_ref, other_ref, out_ref):
+def arrive_body(far, place_ref, mine_ref, *refs):
+    out_ref = refs[-1]
     rows = out_ref.shape[0]
     seq = rows // 2
     half = mine_ref.shape[3]
@@ -427,16 +461,51 @@
     def step(t, _):
         at = pl.multiple_of(t * TILE, TILE)
         where = place_ref[pl.ds(at, TILE), :]
-        lane = iota((TILE, seq), 1)
-        first = one_hot(lane == where)
-        second = one_hot(lane + seq == where)
+        pick = one_hot(iota((TILE, seq), 1) + far * seq == where)
         for side in range(2):
-            a = dot(first, mine_ref[:, side].reshape(seq, half))
-            b = dot(second, other_ref[:, side].reshape(seq, half))
-            out_ref[pl.ds(at, TILE), side * half : (side + 1) * half] = (a + b).astype(BF16)
+            a = dot(pick, mine_ref[:, side].reshape(seq, half))
+            if far:
+                a = a + refs[0][pl.ds(at, TILE), side * half : (side + 1) * half].astype(F32)
+            out_ref[pl.ds(at, TILE), side * half : (side + 1) * half] = a.astype(BF16)
         return 0
 
     lax.fori_loop(0, rows // TILE, step, 0)
+
+
+def chunks_of(ref, bits, to_ref):
+    n, size = ref.shape[0], ref.shape[1]
+    for k in range(n):
+        to_ref[k * size : (k + 1) * size, :] = ref[k ^ bits]
+
+
+def ffn_grads_body(ids_ref, mine_ref, other_ref, up_ref, down_ref, a_ref, b_ref):
+    core, bits = ids_ref[0], ids_ref[2]
+    d, unit = up_ref.shape[0], down_ref.shape[1]
+    unit = up_ref.shape[1] // 2
+    chunks_of(mine_ref, bits, a_ref)
+    chunks_of(other_ref, bits, b_ref)
+    first = core == 0
+    for p in range(2):
+        take = first if p == 0 else jnp.logical_not(first)
+        up = jnp.where(take, a_ref[0:d, :], b_ref[0:d, :])
+        down = jnp.where(take, a_ref[d : 2 * d, :], b_ref[d : 2 * d, :])
+        up_ref[:, p * unit : (p + 1) * unit] = up.astype(F32)
+        down_ref[p * unit : (p + 1) * unit, :] = down.T.astype(F32)
+
+
+def attn_grads_body(ids_ref, mine_ref, other_ref, qkv_ref, out_ref, vec_ref, a_ref, b_ref):
+    core, bits = ids_ref[0], ids_ref[2]
+    d, part = qkv_ref.shape[1], qkv_ref.shape[2] // 2
+    chunks_of(mine_ref, bits, a_ref)
+    chunks_of(other_ref, bits, b_ref)
+    first = core == 0
+    for p in range(2):
+        take = first if p == 0 else jnp.logical_not(first)
+        both = jnp.where(take, a_ref[0:d, :], b_ref[0:d, :])
+        for j in range(3):
+            qkv_ref[j, :, p * part : (p + 1) * part] = both[:, j * part : (j + 1) * part].astype(F32)
+        out_ref[p * part : (p + 1) * part, :] = both[:, 3 * part : 4 * part].T.astype(F32)
+    vec_ref[...] = a_ref[d : d + 16, :].astype(F32)
 
 
 def per_device(
@@ -466,12 +535,18 @@
     device = lax.axis_index("dp")
     core = device % 2
     plane = lax.axis_index("tensor")
-    ids = jnp.stack([core, plane]).astype(jnp.int32)
-    cores = [(i, i ^ 1) for i in range(count)]
+    levels = [1 << b for b in range(1, count.bit_length() - 1)]
+    bits = 0
+    for bit in levels:
+        bits = 2 * bits + (device // bit) % 2
+    ids = jnp.stack([core, plane, bits]).astype(jnp.int32)
     planes = [(0, 1), (1, 0)]
 
+    def across(x, bit):
+        return lax.ppermute(x, "dp", [(i, i ^ bit) for i in range(count)])
+
     def swap_core(x):
-        return lax.ppermute(x, "dp", cores)
+        return across(x, 1)
 
     def swap_plane(x):
         return lax.ppermute(x, "tensor", planes)
@@ -481,6 +556,9 @@
 
     def turn(x):
         return x.reshape(1, -1)
+
+    def after(x, *deps):
+        return lax.optimization_barrier((x, *deps))[0]
 
     slots_row = packed_slot.reshape(1, rows)
     tok_send, place = call(
@@ -491,51 +569,44 @@
         moved=rows * d * 3,
     )(ids, slots_row, tokens)
     tok_mine = trade(tok_send)
+
+    def piece(x, size, axis):
+        return lax.dynamic_slice_in_dim(x, core * size, size, axis=axis)
+
+    qkv_weight_late, out_weight_late, up_late, down_late, bias_late = lax.optimization_barrier(
+        (qkv_weight, out_weight, up_weight, down_weight, up_bias, tok_send)
+    )[:5]
+    out_piece = piece(out_weight_late, part, 0).reshape(part, d // part, part)
+    out_piece = jnp.transpose(out_piece, (1, 0, 2)).reshape(1, d, part)
+    heads_a = swap_plane(jnp.concatenate([piece(qkv_weight_late, part, 2), out_piece], axis=0))
+    bias_own = up_bias.reshape(2, unit)
+    bias_c = piece(bias_late.reshape(2, unit), 1, 0)
+    bias_hi = bias_c.astype(BF16)
+    left = bias_c - bias_hi.astype(F32)
+    bias_mid = left.astype(BF16)
+    bias_lo = (left - bias_mid.astype(F32)).astype(BF16)
+    up_piece = jnp.concatenate(
+        [piece(up_late, unit, 1), bias_hi, bias_mid, bias_lo, jnp.zeros((13, unit), BF16)], axis=0
+    )
+    up_a = swap_plane(up_piece)
+    down_piece = piece(down_late, unit, 0)
+    down_a = swap_plane(down_piece)
+
     grad_send = call(
         send_grads_body,
         shaped((count, slot, half), BF16),
         in_specs=[VMEM, VMEM],
         flops=rows * rows * d,
         moved=rows * d * 3,
-    )(place, out_grad)
-
-    qkv_piece = lax.dynamic_slice_in_dim(qkv_weight, core * part, part, axis=2)
-    bias_own = up_bias.reshape(2, unit)
-    bias_c = lax.dynamic_slice_in_dim(bias_own, core, 1, axis=0)
-    bias_hi = bias_c.astype(BF16)
-    left = bias_c - bias_hi.astype(F32)
-    bias_mid = left.astype(BF16)
-    bias_lo = (left - bias_mid.astype(F32)).astype(BF16)
-    ffn_piece = jnp.concatenate(
-        [
-            lax.dynamic_slice_in_dim(up_weight, core * unit, unit, axis=1),
-            lax.dynamic_slice_in_dim(down_weight, core * unit, unit, axis=0),
-            lax.dynamic_slice_in_dim(out_weight, core * part, part, axis=0),
-            bias_hi,
-            bias_mid,
-            bias_lo,
-            jnp.zeros((13, d), BF16),
-        ],
-        axis=0,
-    )
-    qkv_a = swap_plane(qkv_piece)
-    qkv_b = swap_core(qkv_a)
-    ffn_a = swap_plane(ffn_piece)
-    ffn_b = swap_core(ffn_a)
-
-    def unpack(p):
-        up = p[:d]
-        down = p[d : d + unit]
-        out = p[d + unit : d + unit + part]
-        at = d + unit + part
-        bias = p[at : at + 3].astype(F32)
-        return up, down, out, bias[0:1] + bias[1:2] + bias[2:3]
-
-    up_a, down_a, out_a, bias_a = unpack(ffn_a)
-    up_b, down_b, out_b, bias_b = unpack(ffn_b)
-    bias = jnp.concatenate([bias_own, bias_a, bias_b, jnp.zeros((4, unit), F32)], axis=0)
-
+    )(after(place, heads_a, up_piece, down_piece), out_grad)
+    heads_b = swap_core(heads_a)
+    place_col = place.reshape(rows, 1)
+
+    tok_mine = after(tok_mine, grad_send)
     tok_other = swap_core(tok_mine)
+    grad_mine = trade(after(grad_send, tok_mine))
+    up_b = swap_core(up_a)
+    down_b = swap_core(down_a)
     off = ((device // 2) % (TILE // slot)) * slot
     marks = lax.dynamic_slice_in_dim(tok_mine[:, slot : slot + 2, :], off, slot, axis=2).astype(F32)
     spos = (marks[:, 0] * 128.0 + marks[:, 1]).astype(jnp.int32)
@@ -560,24 +631,26 @@
             pltpu.VMEM((2, width, width), F32),
             pltpu.VMEM((2, 8, width), F32),
         ),
-        in_specs=[SMEM] + [VMEM] * 11,
-        flops=8 * 10**9,
+        in_specs=[SMEM] + [VMEM] * 9,
+        flops=25 * 10**9,
         moved=20 * 10**6,
     )(
-        ids, spos_row, tok_mine, tok_other, qkv_weight, qkv_a, qkv_b, out_weight, out_a, out_b,
+        ids, spos_row, tok_mine, tok_other, qkv_weight, heads_a, heads_b, out_weight,
         turn(gain_first), turn(shift_first),
     )
 
-    grad_mine = trade(grad_send)
+    grad_mine = after(grad_mine, middle)
     grad_other = swap_core(grad_mine)
-
-    out_keep, out_send, dmiddle, ffn_grads, vec2, bvec = call(
+    grad_kind = shaped((2, 2, d, unit), BF16)
+
+    out_keep, out_send, dmiddle, f_keep, f_send, vec2, bvec = call(
         ffn_body,
         (
             shaped((seq, half), BF16),
             shaped((seq, half), BF16),
             shaped((seq, d), F32),
-            shaped((2, 2, 2, d, unit), BF16),
+            grad_kind,
+            grad_kind,
             shaped((8, d), F32),
             shaped((8, unit), F32),
         ),
@@ -588,70 +661,78 @@
             pltpu.VMEM((4, seq, unit), BF16),
         ),
         in_specs=[SMEM] + [VMEM] * 13,
-        flops=16 * 10**9,
+        flops=25 * 10**9,
         moved=20 * 10**6,
     )(
         ids, spos_row, grad_mine, grad_other, middle, up_weight, up_a, up_b,
-        down_weight, down_a, down_b, bias, turn(gain_second), turn(shift_second),
+        down_weight, down_a, down_b, bias_own, turn(gain_second), turn(shift_second),
     )
 
-    place_col = place.reshape(rows, 1)
-
-    def go_back(keep, send):
+    def order(keep, send):
         other = swap_core(send)
-        ordered = call(
+        return call(
             return_body,
             shaped((rows, half), BF16),
             in_specs=[SMEM, VMEM, VMEM, VMEM],
             flops=rows * rows * d,
             moved=rows * d * 3,
-        )(ids, spos_col, keep, other)
-        mine = trade(ordered.reshape(count, slot, half))
+        )(ids, spos_col, keep, other).reshape(count, slot, half)
+
+    def arrive(mine):
         far = swap_plane(mine)
+        shape = (count // 2, 2, slot, half)
+        near = call(
+            functools.partial(arrive_body, 0),
+            shaped((rows, d), BF16),
+            in_specs=[VMEM, VMEM],
+            flops=rows * rows * d,
+            moved=rows * d * 4,
+        )(place_col, mine.reshape(shape))
         return call(
-            arrive_body,
+            functools.partial(arrive_body, 1),
             shaped((rows, d), BF16),
             in_specs=[VMEM, VMEM, VMEM],
-            flops=2 * rows * rows * d,
+            flops=rows * rows * d,
             moved=rows * d * 4,
-        )(place_col, mine.reshape(count // 2, 2, slot, half), far.reshape(count // 2, 2, slot, half))
-
-    layer_out = go_back(out_keep, out_send)
-
-    groups = [[c + 2 * k for k in range(count // 2)] for c in range(2)]
+        )(place_col, far.reshape(shape), near)
 
     def add(a, b):
         return (a.astype(F32) + b.astype(F32)).astype(BF16)
 
-    def reduce(grads, extra):
-        kept, sent = grads[0], grads[1]
-        shape = kept.shape[1:]
-        kept = kept.reshape(2, -1, d)
-        sent = sent.reshape(2, -1, d)
-        n = kept.shape[1]
-        if extra is not None:
-            sent = jnp.concatenate([sent.reshape(2 * n, d), extra], axis=0)
-            kept = jnp.concatenate([kept.reshape(2 * n, d), extra], axis=0)
-        else:
-            sent = sent.reshape(2 * n, d)
-            kept = kept.reshape(2 * n, d)
-        total = add(kept, swap_core(sent))
-        own, far = total[:n], total[n:]
-        if extra is not None:
-            own = jnp.concatenate([own, total[2 * n :]], axis=0)
-        own = add(own, swap_plane(far))
-        own = lax.psum(own, "dp", axis_index_groups=groups)
-        return own[:n].reshape(shape), (own[n:] if extra is not None else None)
-
-    ffn_sum, _ = reduce(ffn_grads, None)
-
-    in_keep, in_send, attn_grads, vec1 = call(
+    def sides(x, bit):
+        high = (device // bit) % 2
+        return (
+            lax.dynamic_index_in_dim(x, high, 0, keepdims=False),
+            lax.dynamic_index_in_dim(x, 1 - high, 0, keepdims=False),
+        )
+
+    def reduce_near(x):
+        kept, sent = sides(x, levels[0])
+        return add(kept, across(sent, levels[0]))
+
+    def reduce_rest(x):
+        for bit in levels[1:]:
+            kept, sent = sides(x.reshape(2, x.shape[0] // 2, x.shape[1]), bit)
+            x = add(kept, across(sent, bit))
+        for bit in reversed(levels):
+            x = jnp.concatenate([x, across(x, bit)], axis=0)
+        return x
+
+    ordered = order(out_keep, out_send)
+    out_mine = trade(ordered)
+    f_total = add(f_keep, swap_core(f_send))
+    f_near = reduce_near(f_total)
+
+    size = 8 * (count // 2)
+    lines = -(-(d + 16) // size) * size
+    piece_kind = shaped((2, 2, lines // 2, 4 * part), BF16)
+    in_keep, in_send, a_keep, a_send = call(
         attend_back_body,
         (
             shaped((seq, half), BF16),
             shaped((seq, half), BF16),
-            shaped((2, 2, d, 4 * part), BF16),
-            shaped((8, d), F32),
+            piece_kind,
+            piece_kind,
         ),
         scratch=(
             pltpu.VMEM((3, d, width), BF16),
@@ -663,47 +744,46 @@
             pltpu.VMEM((3, 2, seq, width), BF16),
             pltpu.VMEM((2, width, width), F32),
             pltpu.VMEM((2, 8, width), F32),
+            pltpu.VMEM((8, d), F32),
         ),
         in_specs=[SMEM] + [VMEM] * 15,
-        flops=12 * 10**9,
+        flops=25 * 10**9,
         moved=20 * 10**6,
     )(
-        ids, dmiddle, out_weight, out_a, out_b, qkv, o, rden, states, zsums,
-        h1, x, qkv_weight, qkv_a, qkv_b, turn(gain_first),
+        ids, after(dmiddle, ordered, f_total), out_weight, qkv, o, rden, states, zsums,
+        h1, x, qkv_weight, heads_a, heads_b, turn(gain_first), vec2, bvec,
     )
-    grad_input = go_back(in_keep, in_send)
-
-    pieces = bvec[:4]
-    ours = pieces[:2]
-    theirs = jnp.where(core == 0, pieces[2:4], pieces[3:1:-1])
-    halves = jnp.where(
-        plane == 0,
-        jnp.concatenate([ours, theirs], axis=0),
-        jnp.concatenate([theirs, ours], axis=0),
-    )
-    extra = jnp.concatenate(
-        [vec1[:2], vec2[:2], halves, jnp.zeros((8, d), F32)], axis=0
-    ).astype(BF16)
-    attn_sum, vec_sum = reduce(attn_grads, extra)
-
-    def both(mine):
-        other = swap_core(mine)
-        return jnp.where(core == 0, mine, other), jnp.where(core == 0, other, mine)
-
-    ffn0, ffn1 = both(ffn_sum)
-    attn0, attn1 = both(attn_sum)
-    grad_up = jnp.concatenate([ffn0[0], ffn1[0]], axis=1).astype(F32)
-    grad_down = jnp.concatenate([ffn0[1].T, ffn1[1].T], axis=0).astype(F32)
-    grad_qkv = jnp.stack(
-        [
-            jnp.concatenate([attn0[:, j * part : (j + 1) * part], attn1[:, j * part : (j + 1) * part]], axis=1)
-            for j in range(3)
-        ]
-    ).astype(F32)
-    grad_outproj = jnp.concatenate([attn0[:, 3 * part :].T, attn1[:, 3 * part :].T], axis=0).astype(F32)
-    vec_sum = vec_sum.astype(F32)
+    in_ordered = order(after(in_keep, out_mine, f_near), in_send)
+    in_mine = trade(in_ordered)
+    f_sum = reduce_rest(add(f_near[0], swap_plane(f_near[1])))
+    a_total = add(after(a_keep, in_ordered), swap_core(a_send))
+    a_near = reduce_near(a_total)
+    a_sum = reduce_rest(add(a_near[0], swap_plane(a_near[1])))
+
+    groups = count // 2
+    f_sum = f_sum.reshape(groups, -1, unit)
+    grad_up, grad_down = call(
+        ffn_grads_body,
+        (shaped((d, 2 * unit), F32), shaped((2 * unit, d), F32)),
+        scratch=(pltpu.VMEM((2 * d, unit), BF16), pltpu.VMEM((2 * d, unit), BF16)),
+        in_specs=[SMEM, VMEM, VMEM],
+        flops=10**9,
+        moved=6 * 10**6,
+    )(ids, f_sum, swap_core(f_sum))
+    a_sum = a_sum.reshape(groups, -1, 4 * part)
+    grad_qkv, grad_outproj, vec_sum = call(
+        attn_grads_body,
+        (shaped((3, d, width), F32), shaped((width, d), F32), shaped((16, d), F32)),
+        scratch=(pltpu.VMEM((lines, 4 * part), BF16), pltpu.VMEM((lines, 4 * part), BF16)),
+        in_specs=[SMEM, VMEM, VMEM],
+        flops=10**9,
+        moved=4 * 10**6,
+    )(ids, a_sum, swap_core(a_sum))
     bias_sum = vec_sum[4:8].reshape(2, 2 * unit)
     grad_up_bias = jnp.where(plane == 0, bias_sum[0], bias_sum[1])
+
+    layer_out = arrive(out_mine)
+    grad_input = arrive(in_mine)
     return (
         layer_out,
         grad_input,

time: 383 us -> 297 us (0.78)
  waiting for transfers between devices: 161 us -> 75.9 us
  local copies, waits for them, and re-layouts: 36.4 us -> 15.2 us
  Pallas kernels: 120 us -> 138 us
  starting transfers between devices: 36.2 us -> 53.1 us
  between operations: 14.4 us -> 1.14 us
    ppermute x6 -> x7, waiting for transfers between devices: 98.9 us -> 11.3 us  [swap_plane(): return lax.ppermute(x, 'tensor', planes)]
    ppermute x10 -> x23, waiting for transfers between devices: 0.13 us -> 61.8 us  [across(): return lax.ppermute(x, 'dp', [(i, i ^ bit) for i in range(count)])]
    psum x1 -> x0, waiting for transfers between devices: 36.2 us -> none  [reduce(): own = lax.psum(own, 'dp', axis_index_groups=groups)]
    all_to_all x4, waiting for transfers between devices: 25.4 us -> 2.79 us  [trade(): return lax.all_to_all(x, 'dp', split_axis=0, concat_axis=0, tiled=True)]
    ppermute x10 -> x23, starting transfers between devices: 2.68 us -> 21.9 us  [across(): return lax.ppermute(x, 'dp', [(i, i ^ bit) for i in range(count)])]
    pallas_call x4 -> x8, Pallas kernels: 31 us -> 48.7 us  [the longest x2 14.9 us: arrive(): call(functools.partial(arrive_body, 1), shaped((rows, d), BF16), in_specs...]
    slice x14 -> x0, local copies, waits for them, and re-layouts: 13.4 us -> none  [the longest x2 6.67 us: reduce(): kept, sent = (grads[0], grads[1])]
    concatenate x4 -> x1, local copies, waits for them, and re-layouts: 8.33 us -> 0.32 us  [per_device(): jnp.concatenate([piece(up_late, unit, 1), bias_hi, bias_mid, bias_lo, jnp...]
  transfers between devices with their start and end apart: 21 -> 34, of which waited for: 8 -> 15; matrix products, arithmetic and copies ran while one was open for 11% -> 7% of each run, Pallas kernels for 14% -> 33%
where the time goes in v2:
time: 297 us; the launch traced here: 296 us
  Pallas kernels  138 us (46%)
  waiting for transfers between devices  75.9 us (26%)
  starting transfers between devices  53.1 us (18%)
  local copies, waits for them, and re-layouts  15.2 us (5%)
  other arithmetic  12.7 us (4%)
    ppermute x23, waiting for transfers between devices, across(): return lax.ppermute(x, 'dp', [(i, i ^ bit) for i in range(count)])  61.8 us
    pallas_call x1, Pallas kernels, per_device(): call(attend_back_body, (shaped((seq, half), BF16), shaped((seq, half), BF...  27.2 us
    pallas_call x1, Pallas kernels, per_device(): call(ffn_body, (shaped((seq, half), BF16), shaped((seq, half), BF16), sha...  25.4 us
    all_to_all x4, starting transfers between devices, trade(): return lax.all_to_all(x, 'dp', split_axis=0, concat_axis=0, tiled=True)  24.5 us
    pallas_call x1, Pallas kernels, per_device(): call(attend_body, (shaped((seq, d), BF16), shaped((seq, d), BF16), shaped...  24.3 us
    ppermute x23, starting transfers between devices, across(): return lax.ppermute(x, 'dp', [(i, i ^ bit) for i in range(count)])  21.9 us
    pallas_call x2, Pallas kernels, arrive(): call(functools.partial(arrive_body, 1), shaped((rows, d), BF16), in_specs...  14.9 us
    pallas_call x2, Pallas kernels, arrive(): call(functools.partial(arrive_body, 0), shaped((rows, d), BF16), in_specs...  14.3 us
  transfers between devices with their start and end apart: 34, of which 15 were waited for; matrix products, arithmetic and copies ran while one was open for 7% of the time, Pallas kernels for 33%

profile of v2, /device:TPU:0, one launch (start us, length us, event | category | flops | bytes accessed | tf_op | source)
XLA Modules:
  0.0 295.7 jit_solution(4910183709013602991)
XLA Ops:
  1.3 6.6 %shard_map.203 = (bf16[16,136,256]{2,1,0:T(8,128)(2,1)}, s32[1,2048]{1,0:T(1,128)}) custom-call(s32[3]{0:T(128)} %pad_add_fusion.ids_ref, s32[1,2048]{1,0:T(1,128)} %bitcast.101, bf16[2048,512]{1,0:T(8,128)(2,1)} %tok_ref.2), custom_call_target="tpu_custom_call" | custom-call | flops 2147483648 | bytes 3145728 | tf_op jit(solution)/shard_map/pallas_call | solution.py:564
  7.9 7.5 %all-to-all-start = ((bf16[16,136,256]{2,1,0:T(8,128)(2,1)}), bf16[16,136,256]{2,1,0:T(8,128)(2,1)S(1)}, u32[]{:S(2)}, u32[]{:S(2)}) async-start(bf16[16,136,256]{2,1,0:T(8,128)(2,1)} %get-tuple-element.50), calls=%async_computation | async-start | bytes 2228224 | tf_op jit(solution)/shard_map/all_to_all | solution.py:555
  15.7 1.0 constant_dynamic-slice_fusion.4
  16.8 1.6 collective-permute-start
  18.8 1.1 constant_dynamic-slice_fusion
  19.9 11.3 %collective-permute-done.wa_ref = bf16[4,512,128]{2,1,0:T(8,128)(2,1)} collective-permute-done((bf16[4,512,128]{2,1,0:T(8,128)(2,1)S(1)}, bf16[4,512,128]{2,1,0:T(8,128)(2,1)}, u32[]{:S(2)}, u32[]{:S(2)}) %collective-permute-start) | collective-permute-done | bytes 524320 | tf_op jit(solution)/shard_map/ppermute | solution.py:552
  31.2 5.4 %shard_map.204 = bf16[16,128,256]{2,1,0:T(8,128)(2,1)} custom-call(s32[1,2048]{1,0:T(1,128)} %get-tuple-element.56.place_ref, bf16[2048,512]{1,0:T(8,128)(2,1)} %tok_ref.3), custom_call_target="tpu_custom_call" | custom-call | flops 2147483648 | bytes 3145728 | tf_op jit(solution)/shard_map/pallas_call | solution.py:595
  36.6 2.8 all-to-all-done.mine_ref
  39.4 0.7 collective-permute-start.1
  40.1 1.5 collective-permute-start.4
  42.2 6.9 %all-to-all-start.1 = ((bf16[16,128,256]{2,1,0:T(8,128)(2,1)}), bf16[16,128,256]{2,1,0:T(8,128)(2,1)S(1)}, u32[]{:S(2)}, u32[]{:S(2)}) async-start(bf16[16,128,256]{2,1,0:T(8,128)(2,1)} %shard_map.204), calls=%async_computation.1 | async-start | bytes 2097152 | tf_op jit(solution)/shard_map/all_to_all | solution.py:555
  49.1 0.6 fusion.12.spos_ref
  49.7 24.3 %shard_map.205 = (bf16[1024,512]{1,0:T(8,128)(2,1)}, bf16[1024,512]{1,0:T(8,128)(2,1)}, bf16[3,2,1024,256]{3,2,1,0:T(8,128)(2,1)}, bf16[2,1024,256]{2,1,0:T(8,12...) custom-call(s32[3]{0:T(128)} %pad_add_fusion.ids_ref, ...), custom_call_target="tpu_custom_call" | custom-call | flops 24999999488 | bytes 20000000 | tf_op jit(solution)/shard_map/pallas_call | solution.py:616
  75.6 2.9 collective-permute-done.7.db_ref
  78.5 0.8 copy-done.14
  79.8 25.4 %shard_map.206 = (bf16[1024,256]{1,0:T(8,128)(2,1)}, bf16[1024,256]{1,0:T(8,128)(2,1)}, f32[1024,512]{1,0:T(8,128)}, bf16[2,2,512,512]{3,2,1,0:T(8,128)(2,1)}, b...) custom-call(s32[3]{0:T(128)} %pad_add_fusion.ids_ref, s32[1,2048]{1,0:T(1,128)} %fusion.12.spos_ref, ...), custom_call_target="tpu_custom_call" | custom-call | flops 24999999488 | bytes 20000000 | tf_op jit(solution)/shard_map/pallas_call | solution.py:646
  105.8 1.4 copy.25.spos_ref
  107.1 3.2 %collective-permute-done.8.other_ref = bf16[1024,256]{1,0:T(8,128)(2,1)S(1)} collective-permute-done((bf16[1024,256]{1,0:T(8,128)(2,1)}, bf16[1024,256]{1,0:T(8,128)(2,1)S(1)}, u32[]{:S(2)}, u32[]{:S(2)}) %collective-permute-start.8) | collective-permute-done | bytes 524320 | tf_op jit(solution)/shard_map/ppermute | solution.py:546
  110.4 0.8 copy-done.15
  111.2 6.4 %shard_map.207 = bf16[2048,256]{1,0:T(8,128)(2,1)} custom-call(s32[3]{0:T(128)} %pad_add_fusion.ids_ref, s32[2048,1]{1,0:T(8,128)} %copy.25.spos_ref, bf16[1024,256]{1,0:T(8,128)(2,1)} %get-tuple-element.61.mine_ref, bf16[1024,256]{1,0:T(8,128)(2,1)} %copy-done.15), custom_call_target="tpu_custom_call" | custom-call | flops 2147483648 | bytes 3145728 | tf_op jit(solution)/shard_map/pallas_call | solution.py:673
  117.6 6.0 %all-to-all-start.2 = ((bf16[16,128,256]{2,1,0:T(8,128)(2,1)}), bf16[16,128,256]{2,1,0:T(8,128)(2,1)}, u32[]{:S(2)}, u32[]{:S(2)}) async-start(bf16[16,128,256]{2,1,0:T(8,128)(2,1)} %bitcast.85), calls=%async_computation.2 | async-start | bytes 2097152 | tf_op jit(solution)/shard_map/all_to_all | solution.py:555
  123.6 1.3 copy-done
  124.9 2.8 add_convert_fusion
  127.9 1.9 collective-permute-start.11
  129.8 27.2 %shard_map.210 = (bf16[1024,256]{1,0:T(8,128)(2,1)}, bf16[1024,256]{1,0:T(8,128)(2,1)}, bf16[2,2,288,512]{3,2,1,0:T(8,128)(2,1)}, bf16[2,2,288,512]{3,2,1,0:T(8,128)(2,1)}) custom-call(s32[3]{0:T(128)} %pad_add_fusion.ids_ref, f32[1024,512]{1,0:T(8,128)} %get-tuple-element.66.dm_ref, bf16[256,512]{1,0:T(8,128)(2,1)} %oown_ref.3, ...), custom_call_target="tpu_custom_call" | custom-call | flops 24999999488 | bytes 20000000 | tf_op jit(solution)/shard_map/pallas_call | solution.py:729
  157.5 3.0 %collective-permute-done.11 = bf16[2,512,512]{2,1,0:T(8,128)(2,1)} collective-permute-done((bf16[2,512,512]{2,1,0:T(8,128)(2,1)S(1)}, bf16[2,512,512]{2,1,0:T(8,128)(2,1)}, u32[]{:S(2)}, u32[]{:S(2)}) %collective-permute-start.11) | collective-permute-done | bytes 1048608 | tf_op jit(solution)/shard_map/ppermute | solution.py:546
  160.5 1.5 fusion
  162.0 0.8 slice_bitcast_fusion
  162.8 1.5 collective-permute-start.23
  164.4 6.4 %shard_map.211 = bf16[2048,256]{1,0:T(8,128)(2,1)} custom-call(s32[3]{0:T(128)} %pad_add_fusion.ids_ref, s32[2048,1]{1,0:T(8,128)} %copy.25.spos_ref, bf16[1024,256]{1,0:T(8,128)(2,1)} %get-tuple-element.77.mine_ref, bf16[1024,256]{1,0:T(8,128)(2,1)} %collective-permute-done.12.other_ref), custom_call_target="tpu_custom_call" | custom-call | flops 2147483648 | bytes 3145728 | tf_op jit(solution)/shard_map/pallas_call | solution.py:673
  170.8 1.6 add_convert_fusion.1
  172.4 0.9 dynamic-slice_bitcast_fusion.1
  173.3 2.0 collective-permute-start.15
  175.3 4.1 %all-to-all-start.3 = ((bf16[16,128,256]{2,1,0:T(8,128)(2,1)}), bf16[16,128,256]{2,1,0:T(8,128)(2,1)S(1)}, u32[]{:S(2)}, u32[]{:S(2)}) async-start(bf16[16,128,256]{2,1,0:T(8,128)(2,1)} %bitcast.19), calls=%async_computation.3 | async-start | bytes 2097152 | tf_op jit(solution)/shard_map/all_to_all | solution.py:555
  179.4 1.2 fusion.2
  180.6 2.0 collective-permute-start.24
  182.6 13.5 %collective-permute-done.15 = bf16[2,288,512]{2,1,0:T(8,128)(2,1)} collective-permute-done((bf16[2,288,512]{2,1,0:T(8,128)(2,1)}, bf16[2,288,512]{2,1,0:T(8,128)(2,1)}, u32[]{:S(2)}, u32[]{:S(2)}) %collective-permute-start.15) | collective-permute-done | bytes 589856 | tf_op jit(solution)/shard_map/ppermute | solution.py:546
  196.1 1.2 fusion.1
  197.9 7.1 %collective-permute-done.24 = bf16[256,512]{1,0:T(8,128)(2,1)S(1)} collective-permute-done((bf16[256,512]{1,0:T(8,128)(2,1)S(1)}, bf16[256,512]{1,0:T(8,128)(2,1)S(1)}, u32[]{:S(2)}, u32[]{:S(2)}) %collective-permute-start.24) | collective-permute-done | bytes 262176 | tf_op jit(solution)/shard_map/ppermute | solution.py:546
  205.1 2.6 collective-permute-start.25
  207.9 6.2 %collective-permute-done.25 = bf16[128,512]{1,0:T(8,128)(2,1)S(1)} collective-permute-done((bf16[128,512]{1,0:T(8,128)(2,1)S(1)}, bf16[128,512]{1,0:T(8,128)(2,1)S(1)}, u32[]{:S(2)}, u32[]{:S(2)}) %collective-permute-start.25) | collective-permute-done | bytes 131104 | tf_op jit(solution)/shard_map/ppermute | solution.py:546
  214.1 1.0 collective-permute-start.26
  215.4 1.8 collective-permute-start.18
  217.2 5.8 %collective-permute-done.26 = bf16[128,512]{1,0:T(8,128)(2,1)S(1)} collective-permute-done((bf16[128,512]{1,0:T(8,128)(2,1)S(1)}, bf16[128,512]{1,0:T(8,128)(2,1)S(1)}, u32[]{:S(2)}, u32[]{:S(2)}) %collective-permute-start.26) | collective-permute-done | bytes 131104 | tf_op jit(solution)/shard_map/ppermute | solution.py:546
  223.1 1.3 collective-permute-done.18
  224.5 0.8 collective-permute-start.19
  225.8 4.7 %collective-permute-done.19 = bf16[72,512]{1,0:T(8,128)(2,1)S(1)} collective-permute-done((bf16[72,512]{1,0:T(8,128)(2,1)S(1)}, bf16[72,512]{1,0:T(8,128)(2,1)S(1)}, u32[]{:S(2)}, u32[]{:S(2)}) %collective-permute-start.19) | collective-permute-done | bytes 73760 | tf_op jit(solution)/shard_map/ppermute | solution.py:546
  230.6 1.8 collective-permute-start.20
  233.0 2.5 collective-permute-start.28
  235.9 2.0 collective-permute-start.21
  237.9 1.4 copy.27.place_ref
  239.3 12.8 %collective-permute-done.21 = bf16[288,512]{1,0:T(8,128)(2,1)S(1)} collective-permute-done((bf16[288,512]{1,0:T(8,128)(2,1)S(1)}, bf16[288,512]{1,0:T(8,128)(2,1)S(1)}, u32[]{:S(2)}, u32[]{:S(2)}) %collective-permute-start.21) | collective-permute-done | bytes 294944 | tf_op jit(solution)/shard_map/ppermute | solution.py:546
  252.0 0.9 pad_maximum_fusion.1
  252.9 1.1 pad_maximum_fusion
  255.1 7.1 %shard_map.208.refs_0_ = bf16[2048,512]{1,0:T(8,128)(2,1)} custom-call(s32[2048,1]{1,0:T(8,128)} %copy.27.place_ref, bf16[8,2,128,256]{3,2,1,0:T(8,128)(2,1)} %bitcast.16.mine_ref), custom_call_target="tpu_custom_call" | custom-call | flops 2147483648 | bytes 4194304 | tf_op jit(solution)/shard_map/pallas_call | solution.py:684
  262.2 7.5 %shard_map.209 = bf16[2048,512]{1,0:T(8,128)(2,1)} custom-call(s32[2048,1]{1,0:T(8,128)} %copy.27.place_ref, bf16[8,2,128,256]{3,2,1,0:T(8,128)(2,1)} %bitcast.15.mine_ref, bf16[2048,512]{1,0:T(8,128)(2,1)} %shard_map.208.refs_0_), custom_call_target="tpu_custom_call" | custom-call | flops 2147483648 | bytes 4194304 | tf_op jit(solution)/shard_map/pallas_call | solution.py:691
  269.7 7.2 %shard_map.212.refs_0_ = bf16[2048,512]{1,0:T(8,128)(2,1)} custom-call(s32[2048,1]{1,0:T(8,128)} %copy.27.place_ref, bf16[8,2,128,256]{3,2,1,0:T(8,128)(2,1)} %bitcast.84), custom_call_target="tpu_custom_call" | custom-call | flops 2147483648 | bytes 4194304 | tf_op jit(solution)/shard_map/pallas_call | solution.py:684
  276.9 0.8 copy-done.12
  277.7 2.7 shard_map.214
  280.4 0.8 select_bitcast_fusion
  281.8 1.5 fusion.11
  283.3 4.0 %shard_map.215 = (f32[512,1024]{1,0:T(8,128)}, f32[1024,512]{1,0:T(8,128)}) custom-call(s32[3]{0:T(128)} %pad_add_fusion.ids_ref, bf16[8,128,512]{2,1,0:T(8,128)(2,1)} %bitcast.87, bf16[8,128,512]{2,1,0:T(8,128)(2,1)} %collective-permute-done.29.other_ref), custom_call_target="tpu_custom_call" | custom-call | flops 1000000000 | bytes 6000000 | tf_op jit(solution)/shard_map/pallas_call | solution.py:765
  287.2 1.0 copy-done.10
  288.2 7.5 %shard_map.213 = bf16[2048,512]{1,0:T(8,128)(2,1)} custom-call(s32[2048,1]{1,0:T(8,128)} %copy.27.place_ref, bf16[8,2,128,256]{3,2,1,0:T(8,128)(2,1)} %bitcast.100, bf16[2048,512]{1,0:T(8,128)(2,1)} %shard_map.212.refs_0_), custom_call_target="tpu_custom_call" | custom-call | flops 2147483648 | bytes 4194304 | tf_op jit(solution)/shard_map/pallas_call | solution.py:691
  (96 shorter events, 9.7 us)
Async XLA Ops:
  7.9 7.5 %copy-start.6 = (bf16[256,512]{1,0:T(8,128)(2,1)S(1)}, bf16[256,512]{1,0:T(8,128)(2,1)}, u32[]{:S(2)}) copy-start(bf16[256,512]{1,0:T(8,128)(2,1)} %oown_ref.3) | copy-start | bytes 786436
  7.9 10.5 %copy-start.8 = (f32[1024]{0:T(1024)S(1)}, f32[1024]{0:T(1024)}, u32[]{:S(2)}) copy-start(f32[1024]{0:T(1024)} %param.24) | copy-start | bytes 12292
  7.9 10.6 %copy-start.7 = (bf16[512,1024]{1,0:T(8,128)(2,1)S(1)}, bf16[512,1024]{1,0:T(8,128)(2,1)}, u32[]{:S(2)}) copy-start(bf16[512,1024]{1,0:T(8,128)(2,1)} %uown_ref.1) | copy-start | bytes 3145732
  7.9 31.5 %all-to-all-start = ((bf16[16,136,256]{2,1,0:T(8,128)(2,1)}), bf16[16,136,256]{2,1,0:T(8,128)(2,1)S(1)}, u32[]{:S(2)}, u32[]{:S(2)}) async-start(bf16[16,136,256]{2,1,0:T(8,128)(2,1)} %get-tuple-element.50), calls=%async_computation | async-start | bytes 2228224 | tf_op jit(solution)/shard_map/all_to_all | solution.py:555
  16.8 14.4 %collective-permute-start = (bf16[4,512,128]{2,1,0:T(8,128)(2,1)S(1)}, bf16[4,512,128]{2,1,0:T(8,128)(2,1)}, u32[]{:S(2)}, u32[]{:S(2)}) collective-permute-start(bf16[4,512,128]{2,1,0:T(8,128)(2,1)S(1)} %pad_maximum_fusion.2), channel_id=1, source_target_pairs={{0,1},{1,0},{2,3},{3,2},{4,5},{5,4},{6,7},{7,6},{8,9},{9,8},{10,11... | collective-permute-start | bytes 1572872 | tf_op jit(solution)/shard_map/ppermute | solution.py:552
  39.4 10.3 %copy-start.2 = (bf16[16,136,256]{2,1,0:T(8,128)(2,1)}, bf16[16,136,256]{2,1,0:T(8,128)(2,1)S(1)}, u32[]{:S(2)}) copy-start(bf16[16,136,256]{2,1,0:T(8,128)(2,1)S(1)} %all-to-all-done.mine_ref) | copy-start | bytes 3342340
  39.4 10.3 %collective-permute-start.1 = (bf16[16,136,256]{2,1,0:T(8,128)(2,1)S(1)}, bf16[16,136,256]{2,1,0:T(8,128)(2,1)}, u32[]{:S(2)}, u32[]{:S(2)}) collective-permute-start(bf16[16,136,256]{2,1,0:T(8,128)(2,1)S(1)} %all-to-all-done.mine_ref), channel_id=1, source_target_pairs={{0,2},{2,0},{4,6},{6,4},{8,10},{10,8},{12,14},{14,12},{16,18},{18,... | collective-permute-start | bytes 3342344 | tf_op jit(solution)/shard_map/ppermute | solution.py:546
  40.1 34.3 %collective-permute-start.4 = (bf16[528,512]{1,0:T(8,128)(2,1)S(1)}, bf16[528,512]{1,0:T(8,128)(2,1)}, u32[]{:S(2)}, u32[]{:S(2)}) collective-permute-start(bf16[528,512]{1,0:T(8,128)(2,1)S(1)} %concatenate.29), channel_id=1, source_target_pairs={{0,1},{1,0},{2,3},{3,2},{4,5},{5,4},{6,7},{7,6},{8,9},{9,8},{10,11... | collective-permute-start | bytes 1622024 | tf_op jit(solution)/shard_map/ppermute | solution.py:552
  41.7 32.9 %collective-permute-start.6 = (bf16[512,512]{1,0:T(8,128)(2,1)S(1)}, bf16[512,512]{1,0:T(8,128)(2,1)}, u32[]{:S(2)}, u32[]{:S(2)}) collective-permute-start(bf16[512,512]{1,0:T(8,128)(2,1)S(1)} %constant_dynamic-slice_fusion), channel_id=1, source_target_pairs={{0,1},{1,0},{2,3},{3,2},{4,5},{5,4},{6,7},{7,6},{8,9},{9,8},{10,11... | collective-permute-start | bytes 1572872 | tf_op jit(solution)/shard_map/ppermute | solution.py:552
  42.2 7.5 %collective-permute-start.2 = (bf16[4,512,128]{2,1,0:T(8,128)(2,1)}, bf16[4,512,128]{2,1,0:T(8,128)(2,1)}, u32[]{:S(2)}, u32[]{:S(2)}) collective-permute-start(bf16[4,512,128]{2,1,0:T(8,128)(2,1)} %collective-permute-done.wa_ref), channel_id=1, source_target_pairs={{0,2},{2,0},{4,6},{6,4},{8,10},{10,8},{12,14},{14,12},{16,18},{18,... | collective-permute-start | bytes 1572872 | tf_op jit(solution)/shard_map/ppermute | solution.py:546
  42.2 31.8 %all-to-all-start.1 = ((bf16[16,128,256]{2,1,0:T(8,128)(2,1)}), bf16[16,128,256]{2,1,0:T(8,128)(2,1)S(1)}, u32[]{:S(2)}, u32[]{:S(2)}) async-start(bf16[16,128,256]{2,1,0:T(8,128)(2,1)} %shard_map.204), calls=%async_computation.1 | async-start | bytes 2097152 | tf_op jit(solution)/shard_map/all_to_all | solution.py:555
  74.0 4.5 %copy-start.4 = (bf16[16,128,256]{2,1,0:T(8,128)(2,1)}, bf16[16,128,256]{2,1,0:T(8,128)(2,1)S(1)}, u32[]{:S(2)}) copy-start(bf16[16,128,256]{2,1,0:T(8,128)(2,1)S(1)} %all-to-all-done.1.mine_ref) | copy-start | bytes 3145732
  74.0 4.5 %collective-permute-start.3 = (bf16[16,128,256]{2,1,0:T(8,128)(2,1)S(1)}, bf16[16,128,256]{2,1,0:T(8,128)(2,1)S(1)}, u32[]{:S(2)}, u32[]{:S(2)}) collective-permute-start(bf16[16,128,256]{2,1,0:T(8,128)(2,1)S(1)} %all-to-all-done.1.mine_ref), channel_id=1, source_target_pairs={{0,2},{2,0},{4,6},{6,4},{8,10},{10,8},{12,14},{14,12},{16,18},{18,... | collective-permute-start | bytes 3145736 | tf_op jit(solution)/shard_map/ppermute | solution.py:546
  74.5 4.0 %collective-permute-start.5 = (bf16[528,512]{1,0:T(8,128)(2,1)}, bf16[528,512]{1,0:T(8,128)(2,1)S(1)}, u32[]{:S(2)}, u32[]{:S(2)}) collective-permute-start(bf16[528,512]{1,0:T(8,128)(2,1)} %collective-permute-done.4.ua_ref), channel_id=1, source_target_pairs={{0,2},{2,0},{4,6},{6,4},{8,10},{10,8},{12,14},{14,12},{16,18},{18,... | collective-permute-start | bytes 1622024 | tf_op jit(solution)/shard_map/ppermute | solution.py:546
  74.6 3.9 %collective-permute-start.7 = (bf16[512,512]{1,0:T(8,128)(2,1)}, bf16[512,512]{1,0:T(8,128)(2,1)S(1)}, u32[]{:S(2)}, u32[]{:S(2)}) collective-permute-start(bf16[512,512]{1,0:T(8,128)(2,1)} %collective-permute-done.6.da_ref), channel_id=1, source_target_pairs={{0,2},{2,0},{4,6},{6,4},{8,10},{10,8},{12,14},{14,12},{16,18},{18,... | collective-permute-start | bytes 1572872 | tf_op jit(solution)/shard_map/ppermute | solution.py:546
  78.5 0.8 copy-start.14
  78.5 1.0 copy-start.13
  78.5 1.3 copy-start.11
  105.3 18.4 %collective-permute-start.10 = (bf16[2,2,512,512]{3,2,1,0:T(8,128)(2,1)}, bf16[2,2,512,512]{3,2,1,0:T(8,128)(2,1)S(1)}, u32[]{:S(2)}, u32[]{:S(2)}) collective-permute-start(bf16[2,2,512,512]{3,2,1,0:T(8,128)(2,1)} %get-tuple-element.65), channel_id=1, source_target_pairs={{0,2},{2,0},{4,6},{6,4},{8,10},{10,8},{12,14},{14,12},{16,18},{18,... | collective-permute-start | bytes 6291464 | tf_op jit(solution)/shard_map/ppermute | solution.py:546
  105.6 4.7 %collective-permute-start.8 = (bf16[1024,256]{1,0:T(8,128)(2,1)}, bf16[1024,256]{1,0:T(8,128)(2,1)S(1)}, u32[]{:S(2)}, u32[]{:S(2)}) collective-permute-start(bf16[1024,256]{1,0:T(8,128)(2,1)} %get-tuple-element.62), channel_id=1, source_target_pairs={{0,2},{2,0},{4,6},{6,4},{8,10},{10,8},{12,14},{14,12},{16,18},{18,... | collective-permute-start | bytes 1572872 | tf_op jit(solution)/shard_map/ppermute | solution.py:546
  110.4 0.8 copy-start.15
  117.6 46.8 %all-to-all-start.2 = ((bf16[16,128,256]{2,1,0:T(8,128)(2,1)}), bf16[16,128,256]{2,1,0:T(8,128)(2,1)}, u32[]{:S(2)}, u32[]{:S(2)}) async-start(bf16[16,128,256]{2,1,0:T(8,128)(2,1)} %bitcast.85), calls=%async_computation.2 | async-start | bytes 2097152 | tf_op jit(solution)/shard_map/all_to_all | solution.py:555
  123.6 1.3 copy-start
  127.9 32.6 %collective-permute-start.11 = (bf16[2,512,512]{2,1,0:T(8,128)(2,1)S(1)}, bf16[2,512,512]{2,1,0:T(8,128)(2,1)}, u32[]{:S(2)}, u32[]{:S(2)}) collective-permute-start(bf16[2,512,512]{2,1,0:T(8,128)(2,1)S(1)} %dynamic-slice_bitcast_fusion), channel_id=1, source_target_pairs={{0,4},{2,6},{4,0},{6,2},{8,12},{10,14},{12,8},{14,10},{16,20},{18,... | collective-permute-start | bytes 3145736 | tf_op jit(solution)/shard_map/ppermute | solution.py:546
  156.9 13.9 %collective-permute-start.14 = (bf16[2,2,288,512]{3,2,1,0:T(8,128)(2,1)}, bf16[2,2,288,512]{3,2,1,0:T(8,128)(2,1)}, u32[]{:S(2)}, u32[]{:S(2)}) collective-permute-start(bf16[2,2,288,512]{3,2,1,0:T(8,128)(2,1)} %get-tuple-element.81), channel_id=1, source_target_pairs={{0,2},{2,0},{4,6},{6,4},{8,10},{10,8},{12,14},{14,12},{16,18},{18,... | collective-permute-start | bytes 3538952 | tf_op jit(solution)/shard_map/ppermute | solution.py:546
  157.0 7.4 %collective-permute-start.12 = (bf16[1024,256]{1,0:T(8,128)(2,1)}, bf16[1024,256]{1,0:T(8,128)(2,1)}, u32[]{:S(2)}, u32[]{:S(2)}) collective-permute-start(bf16[1024,256]{1,0:T(8,128)(2,1)} %get-tuple-element.78), channel_id=1, source_target_pairs={{0,2},{2,0},{4,6},{6,4},{8,10},{10,8},{12,14},{14,12},{16,18},{18,... | collective-permute-start | bytes 1572872 | tf_op jit(solution)/shard_map/ppermute | solution.py:546
  162.8 16.6 %collective-permute-start.23 = (bf16[512,512]{1,0:T(8,128)(2,1)}, bf16[512,512]{1,0:T(8,128)(2,1)}, u32[]{:S(2)}, u32[]{:S(2)}) collective-permute-start(bf16[512,512]{1,0:T(8,128)(2,1)} %slice_bitcast_fusion), channel_id=1, source_target_pairs={{0,1},{1,0},{2,3},{3,2},{4,5},{5,4},{6,7},{7,6},{8,9},{9,8},{10,11... | collective-permute-start | bytes 1572872 | tf_op jit(solution)/shard_map/ppermute | solution.py:552
  164.3 6.5 %copy-start.1 = (bf16[2,2,288,512]{3,2,1,0:T(8,128)(2,1)S(1)}, bf16[2,2,288,512]{3,2,1,0:T(8,128)(2,1)}, u32[]{:S(2)}) copy-start(bf16[2,2,288,512]{3,2,1,0:T(8,128)(2,1)} %get-tuple-element.80) | copy-start | bytes 3538948
  173.3 22.8 %collective-permute-start.15 = (bf16[2,288,512]{2,1,0:T(8,128)(2,1)}, bf16[2,288,512]{2,1,0:T(8,128)(2,1)}, u32[]{:S(2)}, u32[]{:S(2)}) collective-permute-start(bf16[2,288,512]{2,1,0:T(8,128)(2,1)} %dynamic-slice_bitcast_fusion.1), channel_id=1, source_target_pairs={{0,4},{2,6},{4,0},{6,2},{8,12},{10,14},{12,8},{14,10},{16,20},{18,... | collective-permute-start | bytes 1769480 | tf_op jit(solution)/shard_map/ppermute | solution.py:546
  175.3 79.3 %all-to-all-start.3 = ((bf16[16,128,256]{2,1,0:T(8,128)(2,1)}), bf16[16,128,256]{2,1,0:T(8,128)(2,1)S(1)}, u32[]{:S(2)}, u32[]{:S(2)}) async-start(bf16[16,128,256]{2,1,0:T(8,128)(2,1)} %bitcast.19), calls=%async_computation.3 | async-start | bytes 2097152 | tf_op jit(solution)/shard_map/all_to_all | solution.py:555
  180.6 24.4 %collective-permute-start.24 = (bf16[256,512]{1,0:T(8,128)(2,1)S(1)}, bf16[256,512]{1,0:T(8,128)(2,1)S(1)}, u32[]{:S(2)}, u32[]{:S(2)}) collective-permute-start(bf16[256,512]{1,0:T(8,128)(2,1)S(1)} %dynamic-slice_bitcast_fusion.2), channel_id=1, source_target_pairs={{0,8},{2,10},{4,12},{6,14},{8,0},{10,2},{12,4},{14,6},{16,24},{18,... | collective-permute-start | bytes 786440 | tf_op jit(solution)/shard_map/ppermute | solution.py:546
  197.4 10.3 %collective-permute-start.16 = (bf16[288,512]{1,0:T(8,128)(2,1)S(1)}, bf16[288,512]{1,0:T(8,128)(2,1)S(1)}, u32[]{:S(2)}, u32[]{:S(2)}) collective-permute-start(bf16[288,512]{1,0:T(8,128)(2,1)S(1)} %slice_bitcast_fusion.2), channel_id=1, source_target_pairs={{0,1},{1,0},{2,3},{3,2},{4,5},{5,4},{6,7},{7,6},{8,9},{9,8},{10,11... | collective-permute-start | bytes 884744 | tf_op jit(solution)/shard_map/ppermute | solution.py:552
  205.1 8.9 %collective-permute-start.25 = (bf16[128,512]{1,0:T(8,128)(2,1)S(1)}, bf16[128,512]{1,0:T(8,128)(2,1)S(1)}, u32[]{:S(2)}, u32[]{:S(2)}) collective-permute-start(bf16[128,512]{1,0:T(8,128)(2,1)S(1)} %dynamic-slice_bitcast_fusion.4), channel_id=1, source_target_pairs={{0,16},{2,18},{4,20},{6,22},{8,24},{10,26},{12,28},{14,30},{16,0},... | collective-permute-start | bytes 393224 | tf_op jit(solution)/shard_map/ppermute | solution.py:546
  207.8 30.2 %copy-start.9 = (s32[1,2048]{1,0:T(1,128)S(1)}, s32[1,2048]{1,0:T(1,128)}, u32[]{:S(2)}) copy-start(s32[1,2048]{1,0:T(1,128)} %get-tuple-element.56.place_ref) | copy-start | bytes 24580
  207.8 7.5 %collective-permute-start.17 = (bf16[144,512]{1,0:T(8,128)(2,1)S(1)}, bf16[144,512]{1,0:T(8,128)(2,1)S(1)}, u32[]{:S(2)}, u32[]{:S(2)}) collective-permute-start(bf16[144,512]{1,0:T(8,128)(2,1)S(1)} %dynamic-slice_bitcast_fusion.3), channel_id=1, source_target_pairs={{0,8},{2,10},{4,12},{6,14},{8,0},{10,2},{12,4},{14,6},{16,24},{18,... | collective-permute-start | bytes 442376 | tf_op jit(solution)/shard_map/ppermute | solution.py:546
  214.1 9.0 %collective-permute-start.26 = (bf16[128,512]{1,0:T(8,128)(2,1)S(1)}, bf16[128,512]{1,0:T(8,128)(2,1)S(1)}, u32[]{:S(2)}, u32[]{:S(2)}) collective-permute-start(bf16[128,512]{1,0:T(8,128)(2,1)S(1)} %fusion.6), channel_id=1, source_target_pairs={{0,16},{2,18},{4,20},{6,22},{8,24},{10,26},{12,28},{14,30},{16,0},... | collective-permute-start | bytes 393224 | tf_op jit(solution)/shard_map/ppermute | solution.py:546
  215.4 9.1 %collective-permute-start.18 = (bf16[72,512]{1,0:T(8,128)(2,1)S(1)}, bf16[72,512]{1,0:T(8,128)(2,1)S(1)}, u32[]{:S(2)}, u32[]{:S(2)}) collective-permute-start(bf16[72,512]{1,0:T(8,128)(2,1)S(1)} %dynamic-slice_bitcast_fusion.5), channel_id=1, source_target_pairs={{0,16},{2,18},{4,20},{6,22},{8,24},{10,26},{12,28},{14,30},{16,0},... | collective-permute-start | bytes 221192 | tf_op jit(solution)/shard_map/ppermute | solution.py:546
  223.1 9.9 %collective-permute-start.27 = (bf16[256,512]{1,0:T(8,128)(2,1)S(1)}, bf16[256,512]{1,0:T(8,128)(2,1)S(1)}, u32[]{:S(2)}, u32[]{:S(2)}) collective-permute-start(bf16[256,512]{1,0:T(8,128)(2,1)S(1)} %pad_maximum_fusion.5), channel_id=1, source_target_pairs={{0,8},{2,10},{4,12},{6,14},{8,0},{10,2},{12,4},{14,6},{16,24},{18,... | collective-permute-start | bytes 786440 | tf_op jit(solution)/shard_map/ppermute | solution.py:546
  224.5 6.0 %collective-permute-start.19 = (bf16[72,512]{1,0:T(8,128)(2,1)S(1)}, bf16[72,512]{1,0:T(8,128)(2,1)S(1)}, u32[]{:S(2)}, u32[]{:S(2)}) collective-permute-start(bf16[72,512]{1,0:T(8,128)(2,1)S(1)} %fusion.7), channel_id=1, source_target_pairs={{0,16},{2,18},{4,20},{6,22},{8,24},{10,26},{12,28},{14,30},{16,0},... | collective-permute-start | bytes 221192 | tf_op jit(solution)/shard_map/ppermute | solution.py:546
  225.3 36.9 %collective-permute-start.9 = (bf16[16,128,256]{2,1,0:T(8,128)(2,1)}, bf16[16,128,256]{2,1,0:T(8,128)(2,1)}, u32[]{:S(2)}, u32[]{:S(2)}) collective-permute-start(bf16[16,128,256]{2,1,0:T(8,128)(2,1)} %all-to-all-done.2), channel_id=1, source_target_pairs={{0,1},{1,0},{2,3},{3,2},{4,5},{5,4},{6,7},{7,6},{8,9},{9,8},{10,11... | collective-permute-start | bytes 3145736 | tf_op jit(solution)/shard_map/ppermute | solution.py:552
  230.6 5.3 %collective-permute-start.20 = (bf16[144,512]{1,0:T(8,128)(2,1)S(1)}, bf16[144,512]{1,0:T(8,128)(2,1)S(1)}, u32[]{:S(2)}, u32[]{:S(2)}) collective-permute-start(bf16[144,512]{1,0:T(8,128)(2,1)S(1)} %pad_maximum_fusion.6), channel_id=1, source_target_pairs={{0,8},{2,10},{4,12},{6,14},{8,0},{10,2},{12,4},{14,6},{16,24},{18,... | collective-permute-start | bytes 442376 | tf_op jit(solution)/shard_map/ppermute | solution.py:546
  233.0 20.0 %collective-permute-start.28 = (bf16[512,512]{1,0:T(8,128)(2,1)S(1)}, bf16[512,512]{1,0:T(8,128)(2,1)}, u32[]{:S(2)}, u32[]{:S(2)}) collective-permute-start(bf16[512,512]{1,0:T(8,128)(2,1)S(1)} %pad_maximum_fusion.3), channel_id=1, source_target_pairs={{0,4},{2,6},{4,0},{6,2},{8,12},{10,14},{12,8},{14,10},{16,20},{18,... | collective-permute-start | bytes 1572872 | tf_op jit(solution)/shard_map/ppermute | solution.py:546
  235.9 16.1 %collective-permute-start.21 = (bf16[288,512]{1,0:T(8,128)(2,1)S(1)}, bf16[288,512]{1,0:T(8,128)(2,1)S(1)}, u32[]{:S(2)}, u32[]{:S(2)}) collective-permute-start(bf16[288,512]{1,0:T(8,128)(2,1)S(1)} %pad_maximum_fusion.4), channel_id=1, source_target_pairs={{0,4},{2,6},{4,0},{6,2},{8,12},{10,14},{12,8},{14,10},{16,20},{18,... | collective-permute-start | bytes 884744 | tf_op jit(solution)/shard_map/ppermute | solution.py:546
  252.9 24.0 %collective-permute-start.22 = (bf16[8,72,512]{2,1,0:T(8,128)(2,1)}, bf16[8,72,512]{2,1,0:T(8,128)(2,1)S(1)}, u32[]{:S(2)}, u32[]{:S(2)}) collective-permute-start(bf16[8,72,512]{2,1,0:T(8,128)(2,1)} %bitcast.32.mine_ref), channel_id=1, source_target_pairs={{0,2},{2,0},{4,6},{6,4},{8,10},{10,8},{12,14},{14,12},{16,18},{18,... | collective-permute-start | bytes 1769480 | tf_op jit(solution)/shard_map/ppermute | solution.py:546
  254.0 8.2 %copy-start.5 = (bf16[1024,512]{1,0:T(8,128)(2,1)}, bf16[1024,512]{1,0:T(8,128)(2,1)S(1)}, u32[]{:S(2)}) copy-start(bf16[1024,512]{1,0:T(8,128)(2,1)S(1)} %pad_maximum_fusion) | copy-start | bytes 3145732
  254.0 29.2 %collective-permute-start.29 = (bf16[8,128,512]{2,1,0:T(8,128)(2,1)S(1)}, bf16[8,128,512]{2,1,0:T(8,128)(2,1)}, u32[]{:S(2)}, u32[]{:S(2)}) collective-permute-start(bf16[8,128,512]{2,1,0:T(8,128)(2,1)S(1)} %bitcast.86), channel_id=1, source_target_pairs={{0,2},{2,0},{4,6},{6,4},{8,10},{10,8},{12,14},{14,12},{16,18},{18,... | collective-permute-start | bytes 3145736 | tf_op jit(solution)/shard_map/ppermute | solution.py:546
  254.6 7.6 %copy-start.3 = (bf16[16,128,256]{2,1,0:T(8,128)(2,1)}, bf16[16,128,256]{2,1,0:T(8,128)(2,1)S(1)}, u32[]{:S(2)}) copy-start(bf16[16,128,256]{2,1,0:T(8,128)(2,1)S(1)} %all-to-all-done.3) | copy-start | bytes 3145732
  254.6 32.6 %collective-permute-start.13 = (bf16[16,128,256]{2,1,0:T(8,128)(2,1)S(1)}, bf16[16,128,256]{2,1,0:T(8,128)(2,1)S(1)}, u32[]{:S(2)}, u32[]{:S(2)}) collective-permute-start(bf16[16,128,256]{2,1,0:T(8,128)(2,1)S(1)} %all-to-all-done.3), channel_id=1, source_target_pairs={{0,1},{1,0},{2,3},{3,2},{4,5},{5,4},{6,7},{7,6},{8,9},{9,8},{10,11... | collective-permute-start | bytes 3145736 | tf_op jit(solution)/shard_map/ppermute | solution.py:552
  276.9 0.8 copy-start.12
  287.2 1.0 copy-start.10
